TPU v7x, 32 devices: a whole 2x2x4 slice. The times are simulated.
32 devices in a mesh: pix: 16 (over z, y, core), tm: 2 (over x).
Axes of the slice: x: 2, y: 2, z: 4, core: 2. Of those that a mesh axis runs over, the one named last changes fastest.
Arguments:
- iq: bfloat16 [600, 2, 65536], P('tm', None, 'pix'), as said below
- tail_frames: bfloat16 [150, 2, 65536], P(None, None, 'pix'), as said below
- start_basis: float32 [300, 128], replicated, may hold values from -6 to 6
- low_rank: int32 [4], P('tm'), may hold values from 1 to 32
- high_rank: int32 [4], P('tm'), may hold values from 64 to 128
Outputs:
- power: float32 [4, 65536], P('tm', 'pix')
- basis: float32 [4, 300, 128], P('tm')
Inputs may be any that keep to these rules, and one draw needn't show every extreme that they name: low_rank[w] < high_rank[w] <= 128 for every window. `iq`: real-valued samples of order one. `tail_frames`: real-valued samples of order one, continuing iq.
All inputs are finite; a program needn't handle non-finite values.
Results may differ from a plain program's by a relative error of at most 0.0008.
Values may be sent and summed in bfloat16 or wider, within the bound.
A program may use at most 128 MiB of HBM per device.

v0:
```python
import jax
import jax.numpy as jnp
from jax import lax
from jax.sharding import PartitionSpec as P

K = 128
ITERS = 3
WIN_DEV = 2


def from_behind(block, axis, distance):
    devices = range(lax.axis_size(axis))
    route = [(i - distance, i) for i in devices if i - distance in devices]
    return lax.ppermute(block, axis, route)


def iterate(gram, start):
    basis = start
    for step in range(ITERS):
        image = jnp.dot(gram, basis, precision=lax.Precision.HIGHEST)
        inner = jnp.dot(image.T, image, precision=lax.Precision.HIGHEST)
        factor = jnp.linalg.cholesky(inner)
        basis = lax.linalg.triangular_solve(
            factor, image, left_side=False, lower=True, transpose_a=True
        )
    return basis


def body(iq, tail_frames, start_basis, low_rank, high_rank):
    half = iq.shape[0] // WIN_DEV
    width = 2 * half
    incoming = from_behind(iq[:half], "tm", -1)
    at_end = lax.axis_index("tm") == lax.axis_size("tm") - 1
    following = jnp.where(at_end, tail_frames, incoming)
    extended = jnp.concatenate([iq, following], axis=0)
    casoratis = [
        extended[window * half : window * half + width].reshape(width, -1)
        for window in range(WIN_DEV)
    ]
    grams = []
    for matrix in casoratis:
        summed = lax.psum(
            lax.dot_general(
                matrix, matrix, (((1,), (1,)), ((), ())), preferred_element_type=jnp.float32
            ),
            "pix",
        )
        grams.append(summed)
    columns = jnp.arange(K, dtype=jnp.int32)
    powers = []
    bases = []
    for window in range(WIN_DEV):
        basis = iterate(grams[window], start_basis)
        keep = ((columns >= low_rank[window]) & (columns < high_rank[window])).astype(jnp.float32)
        proj = jnp.dot(basis * keep[None, :], basis.T, precision=lax.Precision.HIGHEST).astype(
            jnp.bfloat16
        )
        filtered = jnp.dot(proj, casoratis[window], preferred_element_type=jnp.float32)
        powers.append(jnp.sum((filtered * filtered).reshape(width, 2, -1), axis=(0, 1)) / width)
        bases.append(basis)
    return (jnp.stack(powers), jnp.stack(bases))


def solution(mesh):
    placed = (P("tm", None, "pix"), P(None, None, "pix"), P(), P("tm"), P("tm"))
    return jax.shard_map(
        body,
        mesh=mesh,
        in_specs=placed,
        out_specs=(P("tm", "pix"), P("tm", None, None)),
        check_vma=False,
    )
```

profile of v0, /device:TPU:0, one launch (start us, length us, event | category | flops | bytes accessed | tf_op | source)
XLA Modules:
  0.0 348.0 jit_solution(8615038702145225041)
XLA Ops:
  7.2 4.3 %slice.26 = bf16[150,2,4096]{2,1,0:T(2,128)(2,1)S(1)} slice(bf16[300,2,4096]{2,1,0:T(2,128)(2,1)} %param.8), slice={[0:150], [0:2], [0:4096]} | slice | bytes 4915200 | tf_op jit(solution)/shard_map/slice | solution.py:32
  11.5 1.5 collective-permute-start
  13.0 5.7 %copy.45 = bf16[300,2,4096]{2,0,1:T(8,128)(2,1)} copy(bf16[300,2,4096]{2,1,0:T(2,128)(2,1)S(1)} %copy-done.1) | data formatting | bytes 9830400 | tf_op args[0]
  18.7 15.4 %convolution_bitcast_fusion.1 = f32[300,300]{1,0:T(8,128)} fusion(bf16[300,2,4096]{2,1,0:T(2,128)(2,1)} %param.8), kind=kOutput, calls=%fused_computation.7 | convolution fusion | flops 1474560000 | bytes 5275200 | tf_op jit(solution)/shard_map/dot_general | solution.py:43
  34.1 35.2 %collective-permute-done = bf16[150,2,4096]{2,1,0:T(2,128)(2,1)} collective-permute-done((bf16[150,2,4096]{2,1,0:T(2,128)(2,1)S(1)}, bf16[150,2,4096]{2,1,0:T(2,128)(2,1)}, u32[]{:S(2)}, u32[]{:S(2)}) %collective-permute-start) | collective-permute-done | bytes 2457632 | tf_op jit(solution)/shard_map/ppermute | solution.py:14
  69.3 6.9 %copy_select_fusion = bf16[150,2,4096]{2,0,1:T(8,128)(2,1)S(1)} fusion(bf16[150,2,4096]{2,1,0:T(2,128)(2,1)} %collective-permute-done, bf16[150,2,4096]{2,1,0:T(2,128)(2,1)S(1)} %copy-done.5, pred[]{:T(512)S(6)} %eq.3), kind=kLoop, calls=%fused_computation.3 | loop fusion | flops 1228800 | bytes 7372801 | tf_op jit(solution)/shard_map/jit(_where)/select_n | solution.py:34
  76.2 1.5 pad_maximum_fusion
  77.7 2.2 copy-done.2
  80.0 3.5 %convolution_bitcast_fusion = f32[300,300]{1,0:T(8,128)} fusion(bf16[300,2,4096]{2,0,1:T(8,128)(2,1)S(1)} %pad_maximum_fusion), kind=kOutput, calls=%fused_computation.6 | convolution fusion | flops 1474560000 | bytes 5275200 | tf_op jit(solution)/shard_map/dot_general | solution.py:43
  84.1 10.2 %pad.8 = bf16[304,2,4096]{2,1,0:T(2,128)(2,1)} pad(bf16[300,2,4096]{2,1,0:T(2,128)(2,1)} %param.8, bf16[]{:T(256)} %constant.44), padding=0_4x0_0x0_0 | pad | bytes 9895938
  94.4 10.3 %copy.58 = bf16[38,8,2,4096]{3,1,2,0:T(8,128)(2,1)} copy(bf16[38,8,2,4096]{3,2,1,0:T(2,128)(2,1)} %bitcast.129) | data formatting | bytes 9961472
  107.7 9.9 %copy.56 = bf16[300,2,4096]{2,1,0:T(2,128)(2,1)} copy(bf16[300,2,4096]{2,0,1:T(8,128)(2,1)} %copy-done.2) | data formatting | bytes 9830400 | tf_op jit(solution)/shard_map/slice | solution.py:37
  117.6 9.9 %pad.9 = bf16[304,2,4096]{2,1,0:T(2,128)(2,1)} pad(bf16[300,2,4096]{2,1,0:T(2,128)(2,1)} %copy.56, bf16[]{:T(256)} %constant.44), padding=0_4x0_0x0_0 | pad | bytes 9895938
  127.5 10.6 %copy.59 = bf16[38,8,2,4096]{3,1,2,0:T(8,128)(2,1)} copy(bf16[38,8,2,4096]{3,2,1,0:T(2,128)(2,1)} %bitcast.128) | data formatting | bytes 9961472
  138.1 39.6 %all-reduce.3.cloned.1.call-done = (f32[300,300]{1,0:T(8,128)}, f32[300,300]{1,0:T(8,128)}) async-done(((f32[300,300]{1,0:T(8,128)}, f32[300,300]{1,0:T(8,128)}), (f32[300,300]{1,0:T(8,128)}, f32[300,300]{1,0:T(8,128)})) %all-reduce.3.cloned.1.call-update) | async-done | bytes 720016 | tf_op jit(solution)/shard_map/psum | solution.py:42
  177.6 1.5 fusion.41
  179.8 11.7 %cholesky.137 = f32[128,128]{1,0:T(8,128)S(1)} custom-call(f32[128,128]{1,0:T(8,128)S(1)} %fusion.20), custom_call_target="Cholesky" | custom-call | tf_op jit(solution)/shard_map/jit(cholesky)/cholesky | solution.py:22
  192.8 9.8 %custom-call.13 = f32[1,128,128]{1,2,0:T(8,128)S(1)} custom-call(f32[1,128,128]{2,1,0:T(8,128)S(1)} %fusion.11), custom_call_target="InvertDiagBlocksLowerTriangular" | custom-call | tf_op jit(solution)/shard_map/triangular_solve/custom-call.0 | solution.py:23
  202.9 1.5 fusion.43
  205.1 12.2 %cholesky.148 = f32[128,128]{1,0:T(8,128)S(1)} custom-call(f32[128,128]{1,0:T(8,128)S(1)} %fusion.18), custom_call_target="Cholesky" | custom-call | tf_op jit(solution)/shard_map/jit(cholesky)/cholesky | solution.py:22
  218.6 9.8 %custom-call.14 = f32[1,128,128]{1,2,0:T(8,128)S(1)} custom-call(f32[1,128,128]{2,1,0:T(8,128)S(1)} %fusion.12), custom_call_target="InvertDiagBlocksLowerTriangular" | custom-call | tf_op jit(solution)/shard_map/triangular_solve/custom-call.0 | solution.py:23
  228.7 1.5 fusion.45
  230.9 11.7 %cholesky.159 = f32[128,128]{1,0:T(8,128)S(1)} custom-call(f32[128,128]{1,0:T(8,128)S(1)} %fusion.16), custom_call_target="Cholesky" | custom-call | tf_op jit(solution)/shard_map/jit(cholesky)/cholesky | solution.py:22
  243.9 9.8 %custom-call.15 = f32[1,128,128]{1,2,0:T(8,128)S(1)} custom-call(f32[1,128,128]{2,1,0:T(8,128)S(1)} %fusion.13), custom_call_target="InvertDiagBlocksLowerTriangular" | custom-call | tf_op jit(solution)/shard_map/triangular_solve/custom-call.0 | solution.py:23
  254.8 5.4 %fusion.1 = f32[8192]{0:T(1024)S(1)} fusion(bf16[300,300]{1,0:T(8,128)(2,1)S(1)} %convolution_convert_fusion, bf16[300,8192]{1,0:T(8,128)(2,1)} %bitcast.131), kind=kOutput, calls=%fused_computation.5 | convolution fusion | flops 1479467008 | bytes 5127968 | tf_op jit(solution)/shard_map/dot_general | solution.py:58
  261.5 11.7 %cholesky.104 = f32[128,128]{1,0:T(8,128)S(1)} custom-call(f32[128,128]{1,0:T(8,128)S(1)} %fusion.27), custom_call_target="Cholesky" | custom-call | tf_op jit(solution)/shard_map/jit(cholesky)/cholesky | solution.py:22
  274.5 9.8 %custom-call.10 = f32[1,128,128]{1,2,0:T(8,128)S(1)} custom-call(f32[1,128,128]{2,1,0:T(8,128)S(1)} %fusion.8), custom_call_target="InvertDiagBlocksLowerTriangular" | custom-call | tf_op jit(solution)/shard_map/triangular_solve/custom-call.0 | solution.py:23
  285.8 11.9 %cholesky.115 = f32[128,128]{1,0:T(8,128)S(1)} custom-call(f32[128,128]{1,0:T(8,128)S(1)} %fusion.25), custom_call_target="Cholesky" | custom-call | tf_op jit(solution)/shard_map/jit(cholesky)/cholesky | solution.py:22
  299.0 9.8 %custom-call.11 = f32[1,128,128]{1,2,0:T(8,128)S(1)} custom-call(f32[1,128,128]{2,1,0:T(8,128)S(1)} %fusion.9), custom_call_target="InvertDiagBlocksLowerTriangular" | custom-call | tf_op jit(solution)/shard_map/triangular_solve/custom-call.0 | solution.py:23
  310.3 11.7 %cholesky.126 = f32[128,128]{1,0:T(8,128)S(1)} custom-call(f32[128,128]{1,0:T(8,128)S(1)} %fusion.23), custom_call_target="Cholesky" | custom-call | tf_op jit(solution)/shard_map/jit(cholesky)/cholesky | solution.py:22
  323.3 9.8 %custom-call.12 = f32[1,128,128]{1,2,0:T(8,128)S(1)} custom-call(f32[1,128,128]{2,1,0:T(8,128)S(1)} %fusion.10), custom_call_target="InvertDiagBlocksLowerTriangular" | custom-call | tf_op jit(solution)/shard_map/triangular_solve/custom-call.0 | solution.py:23
  333.9 5.4 %fusion = f32[8192]{0:T(1024)S(1)} fusion(bf16[300,300]{1,0:T(8,128)(2,1)S(1)} %convolution_convert_fusion.1, bf16[300,8192]{1,0:T(8,128)(2,1)} %bitcast.130), kind=kOutput, calls=%fused_computation.4 | convolution fusion | flops 1479467008 | bytes 5127968 | tf_op jit(solution)/shard_map/dot_general | solution.py:58
  (77 shorter events, 21.5 us)
Async XLA Ops:
  7.2 170.4 %copy-start = (f32[300,128]{1,0:T(8,128)S(1)}, f32[300,128]{1,0:T(8,128)}, u32[]{:S(2)}) copy-start(f32[300,128]{1,0:T(8,128)} %param.10) | copy-start | bytes 460804
  7.2 170.4 %all-reduce.3.cloned.1.call-start = ((), (), s32[]{:S(2)}) async-start(), calls=%async_computation | async-start | bytes 1867776 | tf_op jit(solution)/shard_map/psum | solution.py:42
  7.2 5.8 %copy-start.1 = (bf16[300,2,4096]{2,1,0:T(2,128)(2,1)S(1)}, bf16[300,2,4096]{2,1,0:T(2,128)(2,1)}, u32[]{:S(2)}) copy-start(bf16[300,2,4096]{2,1,0:T(2,128)(2,1)} %param.8) | copy-start | bytes 14745604
  11.5 57.8 %collective-permute-start = (bf16[150,2,4096]{2,1,0:T(2,128)(2,1)S(1)}, bf16[150,2,4096]{2,1,0:T(2,128)(2,1)}, u32[]{:S(2)}, u32[]{:S(2)}) collective-permute-start(bf16[150,2,4096]{2,1,0:T(2,128)(2,1)S(1)} %slice.26), channel_id=1, source_target_pairs={{1,0},{3,2},{5,4},{7,6},{9,8},{11,10},{13,12},{15,14},{17,16},{19,... | collective-permute-start | bytes 7372808 | tf_op jit(solution)/shard_map/ppermute | solution.py:14
  18.7 50.6 %copy-start.5 = (bf16[150,2,4096]{2,1,0:T(2,128)(2,1)S(1)}, bf16[150,2,4096]{2,1,0:T(2,128)(2,1)}, u32[]{:S(2)}) copy-start(bf16[150,2,4096]{2,1,0:T(2,128)(2,1)} %param.9) | copy-start | bytes 7372804
  34.1 42.1 %copy-start.3 = (bf16[300,2,4096]{2,0,1:T(8,128)(2,1)S(1)}, bf16[300,2,4096]{2,0,1:T(8,128)(2,1)}, u32[]{:S(2)}) copy-start(bf16[300,2,4096]{2,0,1:T(8,128)(2,1)} %copy.45) | copy-start | bytes 14745604
  77.7 2.3 copy-start.2
  80.0 3.6 %copy-start.6 = (s32[2]{0:T(128)S(1)}, s32[2]{0:T(128)}, u32[]{:S(2)}) copy-start(s32[2]{0:T(128)} %param.12) | copy-start | bytes 28
  94.4 10.3 %copy-start.7 = (s32[2]{0:T(128)S(1)}, s32[2]{0:T(128)}, u32[]{:S(2)}) copy-start(s32[2]{0:T(128)} %param.11) | copy-start | bytes 28
  254.7 5.5 %copy-start.4 = (f32[300,300]{1,0:T(8,128)S(1)}, f32[300,300]{1,0:T(8,128)}, u32[]{:S(2)}) copy-start(f32[300,300]{1,0:T(8,128)} %get-tuple-element.13) | copy-start | bytes 1080004
Sparse Core Ops, SparseCore 0:
  83.6 93.9 all-reduce.2
where the time goes:
time: 351 us; the launch traced here: 348 us
  other arithmetic  149 us (42%)
  waiting for transfers between devices  74.7 us (21%)
  local copies, waits for them, and re-layouts  65.7 us (19%)
  matrix products  41.9 us (12%)
  between operations  14.7 us (4%)
    another operation x18, other arithmetic, iterate(): factor = jnp.linalg.cholesky(inner)  75 us
    another operation x12, other arithmetic, iterate(): lax.linalg.triangular_solve(factor, image, left_side=False, lower=True, t...  62.8 us
    unnamed x22, local copies, waits for them, and re-layouts  49.8 us
    psum x1, waiting for transfers between devices, body(): lax.psum(lax.dot_general(matrix, matrix, (((1,), (1,)), ((), ())), prefer...  39.6 us
    ppermute x1, waiting for transfers between devices, from_behind(): return lax.ppermute(block, axis, route)  35.2 us
    dot_general x2, matrix products, body(): lax.dot_general(matrix, matrix, (((1,), (1,)), ((), ())), preferred_eleme...  19 us
    dot_general x2, matrix products, body(): jnp.dot(proj, casoratis[window], preferred_element_type=jnp.float32)  10.8 us
    slice x1, local copies, waits for them, and re-layouts, body(): extended[window * half:window * half + width].reshape(width, -1)  9.94 us
  transfers between devices with their start and end apart: 2, of which 2 were waited for; matrix products, arithmetic and copies ran while one was open for 22% of the time, Pallas kernels for 0%

commit v1 on v0

v1 whole, which is shorter than its diff:
```python
import functools

import jax
import jax.numpy as jnp
from jax import lax
from jax.experimental import pallas as pl
from jax.experimental.pallas import tpu as pltpu
from jax.sharding import PartitionSpec as P

K = 128
ITERS = 3
WIN_DEV = 2
SUB = 8
HI = lax.Precision.HIGHEST


def from_behind(block, axis, distance):
    devices = range(lax.axis_size(axis))
    route = [(i - distance, i) for i in devices if i - distance in devices]
    return lax.ppermute(block, axis, route)


def dot(a, b, ca, cb):
    return lax.dot_general(
        a, b, (((ca,), (cb,)), ((), ())), precision=HI, preferred_element_type=jnp.float32
    )


def inverse_factors(grams):
    tiles = K // SUB
    lane = lax.broadcasted_iota(jnp.int32, (SUB, K), 1)
    sub = lax.broadcasted_iota(jnp.int32, (SUB, K), 0)
    work = [[m[SUB * u : SUB * u + SUB, :] for u in range(tiles)] for m in grams]
    for j in range(K):
        t, s = divmod(j, SUB)
        here = lane == j
        for rows in work:
            pivot = rows[t][s : s + 1, j : j + 1]
            scaled = jnp.where(here[:1], 1.0, rows[t][s : s + 1, :]) * (1.0 / pivot)
            for u in range(t, tiles):
                if u == t and s == SUB - 1:
                    continue
                column = rows[u][:, j : j + 1]
                update = jnp.where(here, 0.0, rows[u]) - column * scaled
                rows[u] = jnp.where(sub > s, update, rows[u]) if u == t else update
    inverses = []
    for rows in work:
        out = []
        for u in range(tiles):
            row = sub + SUB * u
            diagonal = jnp.sum(jnp.where(lane == row, rows[u], 0.0), axis=1, keepdims=True)
            unit = jnp.where(lane < row, rows[u], jnp.where(lane == row, 1.0, 0.0))
            out.append(unit * lax.rsqrt(diagonal))
        inverses.append(jnp.concatenate(out, axis=0))
    return inverses


def iterate_kernel(low_ref, high_ref, gram_ref, start_ref, basis_ref, proj_ref):
    windows = range(WIN_DEV)
    for window in windows:
        basis_ref[window] = start_ref[...]

    def step(_, carry):
        images = [dot(gram_ref[w], basis_ref[w], 1, 0) for w in windows]
        inverses = inverse_factors([dot(z, z, 0, 0) for z in images])
        for w in windows:
            basis_ref[w] = dot(images[w], inverses[w], 1, 1)
        return carry

    lax.fori_loop(0, ITERS, step, 0)
    columns = lax.broadcasted_iota(jnp.int32, (1, K), 1)
    for w in windows:
        basis = basis_ref[w]
        keep = ((columns >= low_ref[w]) & (columns < high_ref[w])).astype(jnp.float32)
        proj_ref[w] = dot(basis * keep, basis, 1, 1).astype(jnp.bfloat16)


def iterate(grams, start, low, high):
    width = start.shape[0]
    smem = pl.BlockSpec(memory_space=pltpu.SMEM)
    vmem = pl.BlockSpec(memory_space=pltpu.VMEM)
    return pl.pallas_call(
        iterate_kernel,
        out_shape=(
            jax.ShapeDtypeStruct((WIN_DEV, width, K), jnp.float32),
            jax.ShapeDtypeStruct((WIN_DEV, width, width), jnp.bfloat16),
        ),
        in_specs=[smem, smem, vmem, vmem],
        out_specs=(vmem, vmem),
        name="iterate",
    )(low, high, grams, start)


def body(iq, tail_frames, start_basis, low_rank, high_rank):
    half = iq.shape[0] // WIN_DEV
    width = 2 * half
    incoming = from_behind(iq[:half], "tm", -1)
    at_end = lax.axis_index("tm") == lax.axis_size("tm") - 1
    following = jnp.where(at_end, tail_frames, incoming)
    extended = jnp.concatenate([iq, following], axis=0)
    casoratis = [
        extended[window * half : window * half + width].reshape(width, -1)
        for window in range(WIN_DEV)
    ]
    grams = []
    for matrix in casoratis:
        summed = lax.psum(
            lax.dot_general(
                matrix, matrix, (((1,), (1,)), ((), ())), preferred_element_type=jnp.float32
            ),
            "pix",
        )
        grams.append(summed)
    bases, projs = iterate(jnp.stack(grams), start_basis, low_rank, high_rank)
    powers = []
    for window in range(WIN_DEV):
        filtered = jnp.dot(projs[window], casoratis[window], preferred_element_type=jnp.float32)
        powers.append(jnp.sum((filtered * filtered).reshape(width, 2, -1), axis=(0, 1)) / width)
    return (jnp.stack(powers), bases)


def solution(mesh):
    placed = (P("tm", None, "pix"), P(None, None, "pix"), P(), P("tm"), P("tm"))
    return jax.shard_map(
        body,
        mesh=mesh,
        in_specs=placed,
        out_specs=(P("tm", "pix"), P("tm", None, None)),
        check_vma=False,
    )
```

time: 351 us -> 243 us (0.69)
  other arithmetic: 149 us -> 11.3 us
  Pallas kernels: 0 us -> 40.7 us
  matrix products: 41.9 us -> 29.7 us
    another operation x32 -> x2, other arithmetic: 138 us -> 2.82 us  [the longest x1 2.17 us: body(): bases, projs = iterate(jnp.stack(grams), start_basis, low_rank, high_rank)]
    pallas_call x0 -> x1, Pallas kernels: none -> 40.7 us  [iterate(): pl.pallas_call(iterate_kernel, out_shape=(jax.ShapeDtypeStruct((WIN_DEV,...]
    dot_general x16 -> x2, matrix products: 21.1 us -> 10.8 us  [body(): jnp.dot(projs[window], casoratis[window], preferred_element_type=jnp.floa...]
    unnamed x22 -> x18, local copies, waits for them, and re-layouts: 49.8 us -> 49.5 us
  transfers between devices with their start and end apart: 2 -> 2, of which waited for: 2 -> 2; matrix products, arithmetic and copies ran while one was open for 22% -> 30% of each run, Pallas kernels for 0% -> 0%
where the time goes in v1:
time: 243 us; the launch traced here: 240 us
  waiting for transfers between devices  77.9 us (32%)
  local copies, waits for them, and re-layouts  64.1 us (26%)
  Pallas kernels  40.7 us (17%)
  matrix products  29.7 us (12%)
  between operations  14.4 us (6%)
  other arithmetic  11.3 us (5%)
    unnamed x18, local copies, waits for them, and re-layouts  49.5 us
    psum x1, waiting for transfers between devices, body(): lax.psum(lax.dot_general(matrix, matrix, (((1,), (1,)), ((), ())), prefer...  43 us
    pallas_call x1, Pallas kernels, iterate(): pl.pallas_call(iterate_kernel, out_shape=(jax.ShapeDtypeStruct((WIN_DEV,...  40.7 us
    ppermute x1, waiting for transfers between devices, from_behind(): return lax.ppermute(block, axis, route)  34.9 us
    dot_general x2, matrix products, body(): lax.dot_general(matrix, matrix, (((1,), (1,)), ((), ())), preferred_eleme...  18.9 us
    dot_general x2, matrix products, body(): jnp.dot(projs[window], casoratis[window], preferred_element_type=jnp.floa...  10.8 us
    slice x1, local copies, waits for them, and re-layouts, body(): extended[window * half:window * half + width].reshape(width, -1)  10.3 us
    select_n x1, other arithmetic, body(): following = jnp.where(at_end, tail_frames, incoming)  6.91 us
  transfers between devices with their start and end apart: 2, of which 2 were waited for; matrix products, arithmetic and copies ran while one was open for 30% of the time, Pallas kernels for 0%

profile of v1, /device:TPU:0, one launch (start us, length us, event | category | flops | bytes accessed | tf_op | source)
XLA Modules:
  0.0 240.0 jit_solution(3654521889256360726)
XLA Ops:
  7.2 0.0 all-reduce.3.cloned.1.call-start
  7.2 0.0 copy-start
  7.2 4.3 %slice.12 = bf16[150,2,4096]{2,1,0:T(2,128)(2,1)S(1)} slice(bf16[300,2,4096]{2,1,0:T(2,128)(2,1)} %param.5), slice={[0:150], [0:2], [0:4096]} | slice | bytes 4915200 | tf_op jit(solution)/shard_map/slice | solution.py:97
  11.5 1.8 collective-permute-start
  13.3 0.0 copy-done
  13.3 5.7 %copy.27 = bf16[300,2,4096]{2,0,1:T(8,128)(2,1)} copy(bf16[300,2,4096]{2,1,0:T(2,128)(2,1)S(1)} %copy-done) | data formatting | bytes 9830400 | tf_op args[0]
  19.0 0.0 copy-start.3
  19.0 15.4 %convolution_bitcast_fusion.1 = f32[1,300,300]{2,1,0:T(8,128)} fusion(bf16[300,2,4096]{2,1,0:T(2,128)(2,1)} %param.5), kind=kOutput, calls=%fused_computation.7 | convolution fusion | flops 1474560000 | bytes 5275200 | tf_op jit(solution)/shard_map/dot_general | solution.py:108
  34.4 34.9 %collective-permute-done = bf16[150,2,4096]{2,1,0:T(2,128)(2,1)} collective-permute-done((bf16[150,2,4096]{2,1,0:T(2,128)(2,1)S(1)}, bf16[150,2,4096]{2,1,0:T(2,128)(2,1)}, u32[]{:S(2)}, u32[]{:S(2)}) %collective-permute-start) | collective-permute-done | bytes 2457632 | tf_op jit(solution)/shard_map/ppermute | solution.py:20
  69.3 0.0 copy-done.3
  69.3 6.9 %copy_select_fusion = bf16[150,2,4096]{2,0,1:T(8,128)(2,1)S(1)} fusion(bf16[150,2,4096]{2,1,0:T(2,128)(2,1)} %collective-permute-done, bf16[150,2,4096]{2,1,0:T(2,128)(2,1)S(1)} %copy-done.3, pred[]{:T(512)S(6)} %eq.3), kind=kLoop, calls=%fused_computation.3 | loop fusion | flops 1228800 | bytes 7372801 | tf_op jit(solution)/shard_map/jit(_where)/select_n | solution.py:99
  76.2 0.0 copy-done.2
  76.2 1.5 pad_maximum_fusion
  77.7 0.0 copy-start.1
  77.7 2.2 copy-done.1
  80.0 3.5 %convolution_bitcast_fusion = f32[1,300,300]{2,1,0:T(8,128)} fusion(bf16[300,2,4096]{2,0,1:T(8,128)(2,1)S(1)} %pad_maximum_fusion), kind=kOutput, calls=%fused_computation.6 | convolution fusion | flops 1474560000 | bytes 5275200 | tf_op jit(solution)/shard_map/dot_general | solution.py:108
  83.5 0.0 all-reduce.3.cloned.1.call-update
  83.5 10.1 %pad.8 = bf16[304,2,4096]{2,1,0:T(2,128)(2,1)} pad(bf16[300,2,4096]{2,1,0:T(2,128)(2,1)} %param.5, bf16[]{:T(256)} %constant.15), padding=0_4x0_0x0_0 | pad | bytes 9895938
  93.6 10.3 %copy.34 = bf16[38,8,2,4096]{3,1,2,0:T(8,128)(2,1)} copy(bf16[38,8,2,4096]{3,2,1,0:T(2,128)(2,1)} %bitcast.25) | data formatting | bytes 9961472
  103.9 10.3 %copy.32 = bf16[300,2,4096]{2,1,0:T(2,128)(2,1)} copy(bf16[300,2,4096]{2,0,1:T(8,128)(2,1)} %copy-done.1) | data formatting | bytes 9830400 | tf_op jit(solution)/shard_map/slice | solution.py:102
  114.2 9.8 %pad.9 = bf16[304,2,4096]{2,1,0:T(2,128)(2,1)} pad(bf16[300,2,4096]{2,1,0:T(2,128)(2,1)} %copy.32, bf16[]{:T(256)} %constant.15), padding=0_4x0_0x0_0 | pad | bytes 9895938
  124.0 10.5 %copy.35 = bf16[38,8,2,4096]{3,1,2,0:T(8,128)(2,1)} copy(bf16[38,8,2,4096]{3,2,1,0:T(2,128)(2,1)} %bitcast.24) | data formatting | bytes 9961472
  134.5 43.0 %all-reduce.3.cloned.1.call-done = (f32[1,300,300]{2,1,0:T(8,128)}, f32[1,300,300]{2,1,0:T(8,128)}) async-done(((f32[1,300,300]{2,1,0:T(8,128)}, f32[1,300,300]{2,1,0:T(8,128)}), (f32[1,300,300]{2,1,0:T(8,128)}, f32[1,300,300]{2,1,0:T(8,128)})) %all-reduce.3.cloned.1.call-update) | async-done | bytes 720016 | tf_op jit(solution)/shard_map/psum | solution.py:107
  177.5 2.2 pad_maximum_fusion.1.gram_ref
  179.7 40.7 %iterate.1 = (f32[2,300,128]{2,1,0:T(8,128)}, bf16[2,300,300]{2,1,0:T(8,128)(2,1)}) custom-call(s32[2]{0:T(128)} %low_ref.1, s32[2]{0:T(128)} %high_ref.1, f32[2,300,300]{2,1,0:T(8,128)} %pad_maximum_fusion.1.gram_ref, f32[300,128]{1,0:T(8,128)} %start_ref.1), custom_call_target="tpu_custom_call" | custom-call | tf_op jit(solution)/shard_map/iterate/pallas_call | solution.py:82
  220.4 5.3 %fusion.1 = f32[8192]{0:T(1024)S(1)} fusion(bf16[300,8192]{1,0:T(8,128)(2,1)} %bitcast.27, bf16[2,300,300]{2,1,0:T(8,128)(2,1)} %get-tuple-element.4), kind=kOutput, calls=%fused_computation.5 | convolution fusion | flops 1479467008 | bytes 5246976 | tf_op jit(solution)/shard_map/dot_general | solution.py:117
  225.9 0.0 copy-done.5
  225.9 0.0 copy-start.4
  225.9 5.4 %fusion = f32[8192]{0:T(1024)S(1)} fusion(bf16[300,8192]{1,0:T(8,128)(2,1)} %bitcast.26, bf16[2,300,300]{2,1,0:T(8,128)(2,1)S(1)} %copy-done.5), kind=kOutput, calls=%fused_computation.4 | convolution fusion | flops 1479467008 | bytes 5181440 | tf_op jit(solution)/shard_map/dot_general | solution.py:117
  231.4 0.0 copy-done.4
  231.4 0.9 copy.33
  232.3 0.6 pad_maximum_fusion.2
  (8 shorter events, 0.1 us)
Async XLA Ops:
  7.2 170.4 %all-reduce.3.cloned.1.call-start = ((), (), s32[]{:S(2)}) async-start(), calls=%async_computation | async-start | bytes 1867776 | tf_op jit(solution)/shard_map/psum | solution.py:107
  7.2 6.1 %copy-start = (bf16[300,2,4096]{2,1,0:T(2,128)(2,1)S(1)}, bf16[300,2,4096]{2,1,0:T(2,128)(2,1)}, u32[]{:S(2)}) copy-start(bf16[300,2,4096]{2,1,0:T(2,128)(2,1)} %param.5) | copy-start | bytes 14745604
  11.5 57.8 %collective-permute-start = (bf16[150,2,4096]{2,1,0:T(2,128)(2,1)S(1)}, bf16[150,2,4096]{2,1,0:T(2,128)(2,1)}, u32[]{:S(2)}, u32[]{:S(2)}) collective-permute-start(bf16[150,2,4096]{2,1,0:T(2,128)(2,1)S(1)} %slice.12), channel_id=1, source_target_pairs={{1,0},{3,2},{5,4},{7,6},{9,8},{11,10},{13,12},{15,14},{17,16},{19,... | collective-permute-start | bytes 7372808 | tf_op jit(solution)/shard_map/ppermute | solution.py:20
  19.0 50.3 %copy-start.3 = (bf16[150,2,4096]{2,1,0:T(2,128)(2,1)S(1)}, bf16[150,2,4096]{2,1,0:T(2,128)(2,1)}, u32[]{:S(2)}) copy-start(bf16[150,2,4096]{2,1,0:T(2,128)(2,1)} %param.6) | copy-start | bytes 7372804
  34.3 41.8 %copy-start.2 = (bf16[300,2,4096]{2,0,1:T(8,128)(2,1)S(1)}, bf16[300,2,4096]{2,0,1:T(8,128)(2,1)}, u32[]{:S(2)}) copy-start(bf16[300,2,4096]{2,0,1:T(8,128)(2,1)} %copy.27) | copy-start | bytes 14745604
  77.7 2.3 copy-start.1
  220.4 5.4 %copy-start.5 = (bf16[2,300,300]{2,1,0:T(8,128)(2,1)S(1)}, bf16[2,300,300]{2,1,0:T(8,128)(2,1)}, u32[]{:S(2)}) copy-start(bf16[2,300,300]{2,1,0:T(8,128)(2,1)} %get-tuple-element.4) | copy-start | bytes 1080004
  225.9 5.5 %copy-start.4 = (f32[2,300,128]{2,1,0:T(8,128)S(1)}, f32[2,300,128]{2,1,0:T(8,128)}, u32[]{:S(2)}) copy-start(f32[2,300,128]{2,1,0:T(8,128)} %get-tuple-element.13) | copy-start | bytes 921604
Sparse Core Ops, SparseCore 0:
  83.6 93.8 all-reduce.2

commit v2 on v1

v2 whole, which is shorter than its diff:
```python
import functools

import jax
import jax.numpy as jnp
from jax import lax
from jax.experimental import pallas as pl
from jax.experimental.pallas import tpu as pltpu
from jax.sharding import PartitionSpec as P

K = 128
ITERS = 3
WIN_DEV = 2
SUB = 8
LANES = 128
BLOCKS = 5
HI = lax.Precision.HIGHEST
MESH = pl.DeviceIdType.MESH
VMEM = pl.BlockSpec(memory_space=pltpu.VMEM)
SMEM = pl.BlockSpec(memory_space=pltpu.SMEM)


def from_behind(block, axis, distance):
    devices = range(lax.axis_size(axis))
    route = [(i - distance, i) for i in devices if i - distance in devices]
    return lax.ppermute(block, axis, route)


def dot(a, b, ca, cb, precision=HI):
    return lax.dot_general(
        a, b, (((ca,), (cb,)), ((), ())), precision=precision, preferred_element_type=jnp.float32
    )


def up(value, unit):
    return -(-value // unit) * unit


def gram_kernel(half, own_ref, next_ref, packed_ref, acc):
    step = pl.program_id(0)

    @pl.when(step == 0)
    def _():
        acc[...] = jnp.zeros_like(acc)

    first, second, third = own_ref[0], own_ref[1], next_ref[...]
    pairs = ((first, first), (first, second), (second, second), (second, third), (third, third))
    for k, (a, b) in enumerate(pairs):
        acc[k] += dot(a, b, 1, 1, None)

    @pl.when(step == pl.num_programs(0) - 1)
    def _():
        pitch = up(half, SUB)
        packed_ref[...] = jnp.zeros_like(packed_ref)
        for k in range(BLOCKS):
            packed_ref[pitch * k : pitch * k + half] = acc[k, :, :LANES]
        rest = [acc[k, :, LANES:] for k in range(BLOCKS)]
        rest.append(jnp.zeros((half, LANES - BLOCKS * (half - LANES)), jnp.float32))
        packed_ref[pitch * BLOCKS : pitch * BLOCKS + half] = jnp.concatenate(rest, axis=1)


def gram_blocks(own, following, rows):
    _, half, columns = own.shape
    tile = 1024
    return pl.pallas_call(
        functools.partial(gram_kernel, half),
        out_shape=jax.ShapeDtypeStruct((rows, LANES), jnp.float32),
        grid=(columns // tile,),
        in_specs=[
            pl.BlockSpec((2, half, tile), lambda i: (0, 0, i)),
            pl.BlockSpec((half, tile), lambda i: (0, i)),
        ],
        out_specs=pl.BlockSpec((rows, LANES), lambda i: (0, 0)),
        scratch_shapes=[pltpu.VMEM((BLOCKS, half, half), jnp.float32)],
        name="gram",
    )(own, following)


def sum_kernel(n, x_ref, out_ref, acc, landed, gathered, send_sem, recv_sem):
    me = lax.axis_index("pix")
    bits = n.bit_length() - 1
    bit = [lax.rem(me // (1 << b), 2) for b in range(bits)]
    partner = [me + (1 - 2 * bit[b]) * (1 << b) for b in range(bits)]

    barrier = pltpu.get_barrier_semaphore()
    for b in range(bits):
        pl.semaphore_signal(
            barrier, inc=1, device_id={"pix": partner[b]}, device_id_type=MESH
        )
    pl.semaphore_wait(barrier, bits)

    def window(start, size):
        return pl.ds(pl.multiple_of(start, SUB), size)

    start, size, base = 0, x_ref.shape[0], 0
    for b in range(bits):
        size //= 2
        keep = start + bit[b] * size
        give = start + (1 - bit[b]) * size
        source = x_ref if b == 0 else acc
        copy = pltpu.make_async_remote_copy(
            src_ref=source.at[window(give, size)],
            dst_ref=landed.at[pl.ds(base, size)],
            send_sem=send_sem.at[b],
            recv_sem=recv_sem.at[b],
            device_id={"pix": partner[b]},
            device_id_type=MESH,
        )
        copy.start()
        copy.wait()
        target = gathered if b == bits - 1 else acc
        target[window(keep, size)] = source[window(keep, size)] + landed[pl.ds(base, size)]
        start, base = keep, base + size
    for b in reversed(range(bits)):
        copy = pltpu.make_async_remote_copy(
            src_ref=gathered.at[window(start, size)],
            dst_ref=gathered.at[window(start, size)],
            send_sem=send_sem.at[bits + b],
            recv_sem=recv_sem.at[bits + b],
            device_id={"pix": partner[b]},
            device_id_type=MESH,
        )
        copy.start()
        copy.wait()
        start, size = start - bit[b] * size, 2 * size
    out_ref[...] = gathered[...]


def sum_over_pix(packed):
    n = lax.axis_size("pix")
    bits = n.bit_length() - 1
    return pl.pallas_call(
        functools.partial(sum_kernel, n),
        out_shape=jax.ShapeDtypeStruct(packed.shape, jnp.float32),
        in_specs=[VMEM],
        out_specs=VMEM,
        scratch_shapes=[
            pltpu.VMEM(packed.shape, jnp.float32),
            pltpu.VMEM(packed.shape, jnp.float32),
            pltpu.VMEM(packed.shape, jnp.float32),
            pltpu.SemaphoreType.DMA((2 * bits,)),
            pltpu.SemaphoreType.DMA((2 * bits,)),
        ],
        compiler_params=pltpu.CompilerParams(collective_id=0, has_side_effects=True),
        name="sum_over_pix",
    )(packed)


def inverse_factors(grams):
    tiles = K // SUB
    lane = lax.broadcasted_iota(jnp.int32, (SUB, K), 1)
    sub = lax.broadcasted_iota(jnp.int32, (SUB, K), 0)
    work = [[m[SUB * u : SUB * u + SUB, :] for u in range(tiles)] for m in grams]
    for j in range(K):
        t, s = divmod(j, SUB)
        here = lane == j
        for rows in work:
            pivot = rows[t][s : s + 1, j : j + 1]
            scaled = jnp.where(here[:1], 1.0, rows[t][s : s + 1, :]) * (1.0 / pivot)
            for u in range(t, tiles):
                if u == t and s == SUB - 1:
                    continue
                column = rows[u][:, j : j + 1]
                update = jnp.where(here, 0.0, rows[u]) - column * scaled
                rows[u] = jnp.where(sub > s, update, rows[u]) if u == t else update
    inverses = []
    for rows in work:
        out = []
        for u in range(tiles):
            row = sub + SUB * u
            diagonal = jnp.sum(jnp.where(lane == row, rows[u], 0.0), axis=1, keepdims=True)
            unit = jnp.where(lane < row, rows[u], jnp.where(lane == row, 1.0, 0.0))
            out.append(unit * lax.rsqrt(diagonal))
        inverses.append(jnp.concatenate(out, axis=0))
    return inverses


def iterate_kernel(half, low_ref, high_ref, packed_ref, start_ref, basis_ref, proj_ref, gram, held):
    windows = range(WIN_DEV)
    pitch = up(half, SUB)
    extra = half - LANES
    for k in range(BLOCKS):
        gram[k, :, :LANES] = packed_ref[pitch * k : pitch * k + half]
        gram[k, :, LANES:] = packed_ref[
            pitch * BLOCKS : pitch * BLOCKS + half, extra * k : extra * k + extra
        ]
    for w in windows:
        held[w, 0] = start_ref[:half]
        held[w, 1] = start_ref[half:]

    def step(_, carry):
        images = []
        for w in windows:
            top, cross, low = gram[2 * w], gram[2 * w + 1], gram[2 * w + 2]
            above, below = held[w, 0], held[w, 1]
            images.append(
                (
                    dot(top, above, 1, 0) + dot(cross, below, 1, 0),
                    dot(cross, above, 0, 0) + dot(low, below, 1, 0),
                )
            )
        inverses = inverse_factors([dot(a, a, 0, 0) + dot(b, b, 0, 0) for a, b in images])
        for w in windows:
            for h in range(2):
                held[w, h] = dot(images[w][h], inverses[w], 1, 1)
        return carry

    lax.fori_loop(0, ITERS, step, 0)
    columns = lax.broadcasted_iota(jnp.int32, (1, K), 1)
    for w in windows:
        keep = ((columns >= low_ref[w]) & (columns < high_ref[w])).astype(jnp.float32)
        basis_ref[w, :half] = held[w, 0]
        basis_ref[w, half:] = held[w, 1]
        for i in range(2):
            for j in range(2):
                proj_ref[w, i, j] = dot(held[w, i] * keep, held[w, j], 1, 1).astype(jnp.bfloat16)


def iterate(packed, start, low, high):
    half = start.shape[0] // 2
    return pl.pallas_call(
        functools.partial(iterate_kernel, half),
        out_shape=(
            jax.ShapeDtypeStruct((WIN_DEV, 2 * half, K), jnp.float32),
            jax.ShapeDtypeStruct((WIN_DEV, 2, 2, half, half), jnp.bfloat16),
        ),
        in_specs=[SMEM, SMEM, VMEM, VMEM],
        out_specs=(VMEM, VMEM),
        scratch_shapes=[
            pltpu.VMEM((BLOCKS, half, half), jnp.float32),
            pltpu.VMEM((WIN_DEV, 2, half, K), jnp.float32),
        ],
        name="iterate",
    )(low, high, packed, start)


def filter_kernel(half, proj_ref, *refs):
    own, following, power_ref = refs[:2], refs[2:4], refs[4]
    for w in range(WIN_DEV):
        total = 0.0
        for part in range(2):
            above = own[part][w]
            below = own[part][1] if w == 0 else following[part][...]
            for i in range(2):
                rows = dot(proj_ref[w, i, 0], above, 1, 0, None)
                rows += dot(proj_ref[w, i, 1], below, 1, 0, None)
                total += jnp.sum(rows * rows, axis=0, keepdims=True)
        power_ref[w : w + 1] = total / (2 * half)


def filtered_power(projs, own, following):
    _, half, columns = own.shape
    pixels = columns // 2
    tile = 512
    count = pixels // tile
    return pl.pallas_call(
        functools.partial(filter_kernel, half),
        out_shape=jax.ShapeDtypeStruct((WIN_DEV, pixels), jnp.float32),
        grid=(count,),
        in_specs=[
            pl.BlockSpec(projs.shape, lambda i: (0, 0, 0, 0, 0)),
            pl.BlockSpec((2, half, tile), lambda i: (0, 0, i)),
            pl.BlockSpec((2, half, tile), lambda i: (0, 0, i + count)),
            pl.BlockSpec((half, tile), lambda i: (0, i)),
            pl.BlockSpec((half, tile), lambda i: (0, i + count)),
        ],
        out_specs=pl.BlockSpec((WIN_DEV, tile), lambda i: (0, i)),
        name="filter",
    )(projs, own, own, following, following)


def body(iq, tail_frames, start_basis, low_rank, high_rank):
    half = iq.shape[0] // WIN_DEV
    incoming = from_behind(iq[:half], "tm", -1)
    at_end = lax.axis_index("tm") == lax.axis_size("tm") - 1
    following = jnp.where(at_end, tail_frames, incoming).reshape(half, -1)
    own = iq.reshape(WIN_DEV, half, -1)
    rows = up(up(half, SUB) * (BLOCKS + 1), SUB * lax.axis_size("pix"))
    packed = sum_over_pix(gram_blocks(own, following, rows))
    bases, projs = iterate(packed, start_basis, low_rank, high_rank)
    return (filtered_power(projs, own, following), bases)


def solution(mesh):
    placed = (P("tm", None, "pix"), P(None, None, "pix"), P(), P("tm"), P("tm"))
    return jax.shard_map(
        body,
        mesh=mesh,
        in_specs=placed,
        out_specs=(P("tm", "pix"), P("tm", None, None)),
        check_vma=False,
    )
```

time: 243 us -> 166 us (0.68)
  Pallas kernels: 40.7 us -> 92.2 us
  local copies, waits for them, and re-layouts: 64.1 us -> 16.7 us
  matrix products: 29.7 us -> 0 us
  waiting for transfers between devices: 77.9 us -> 50.3 us
  between operations: 14.4 us -> 0.67 us
  other arithmetic: 11.3 us -> 4.23 us
    pallas_call x1 -> x4, Pallas kernels: 40.7 us -> 92.2 us  [the longest x1 43.2 us: iterate(): pl.pallas_call(functools.partial(iterate_kernel, half), out_shape=(jax.Sh...]
    unnamed x18 -> x5, local copies, waits for them, and re-layouts: 49.5 us -> 6.48 us
    psum x1 -> x0, waiting for transfers between devices: 43 us -> none  [body(): lax.psum(lax.dot_general(matrix, matrix, (((1,), (1,)), ((), ())), prefer...]
    dot_general x4 -> x0, matrix products: 29.7 us -> none  [the longest x2 18.9 us: body(): lax.dot_general(matrix, matrix, (((1,), (1,)), ((), ())), preferred_eleme...]
    ppermute x1, waiting for transfers between devices: 34.9 us -> 50.3 us  [from_behind(): return lax.ppermute(block, axis, route)]
    slice x1 -> x0, local copies, waits for them, and re-layouts: 10.3 us -> none  [body(): extended[window * half:window * half + width].reshape(width, -1)]
    reshape x0 -> x1, local copies, waits for them, and re-layouts: none -> 6.16 us  [body(): own = iq.reshape(WIN_DEV, half, -1)]
    another operation x2 -> x0, other arithmetic: 2.82 us -> none  [the longest x1 2.17 us: body(): bases, projs = iterate(jnp.stack(grams), start_basis, low_rank, high_rank)]
  transfers between devices with their start and end apart: 2 -> 1, of which waited for: 2 -> 1; matrix products, arithmetic and copies ran while one was open for 30% -> 4% of each run, Pallas kernels for 0% -> 0%
where the time goes in v2:
time: 166 us; the launch traced here: 165 us
  Pallas kernels  92.2 us (56%)
  waiting for transfers between devices  50.3 us (30%)
  local copies, waits for them, and re-layouts  16.7 us (10%)
  other arithmetic  4.23 us (3%)
    ppermute x1, waiting for transfers between devices, from_behind(): return lax.ppermute(block, axis, route)  50.3 us
    pallas_call x1, Pallas kernels, iterate(): pl.pallas_call(functools.partial(iterate_kernel, half), out_shape=(jax.Sh...  43.2 us
    pallas_call x1, Pallas kernels, sum_over_pix(): pl.pallas_call(functools.partial(sum_kernel, n), out_shape=jax.ShapeDtype...  30.1 us
    pallas_call x1, Pallas kernels, filtered_power(): pl.pallas_call(functools.partial(filter_kernel, half), out_shape=jax.Shap...  10 us
    pallas_call x1, Pallas kernels, gram_blocks(): pl.pallas_call(functools.partial(gram_kernel, half), out_shape=jax.ShapeD...  8.9 us
    unnamed x5, local copies, waits for them, and re-layouts  6.48 us
    reshape x1, local copies, waits for them, and re-layouts, body(): own = iq.reshape(WIN_DEV, half, -1)  6.16 us
    select_n x1, other arithmetic, body(): following = jnp.where(at_end, tail_frames, incoming).reshape(half, -1)  4.23 us
  transfers between devices with their start and end apart: 1, of which 1 were waited for; matrix products, arithmetic and copies ran while one was open for 4% of the time, Pallas kernels for 0%

profile of v2, /device:TPU:0, one launch (start us, length us, event | category | flops | bytes accessed | tf_op | source)
XLA Modules:
  0.0 165.4 jit_solution(2372133745008878395)
XLA Ops:
  0.6 4.1 %slice.3 = bf16[150,2,4096]{2,1,0:T(2,128)(2,1)S(1)} slice(bf16[300,2,4096]{2,1,0:T(2,128)(2,1)} %param.5), slice={[0:150], [0:2], [0:4096]} | slice | bytes 4915200 | tf_op jit(solution)/shard_map/slice | solution.py:273
  4.7 1.3 collective-permute-start
  6.0 6.2 %reshape.10.own_ref.refs_0_.refs_1_ = bf16[2,150,8192]{2,1,0:T(8,128)(2,1)} reshape(bf16[300,2,4096]{2,1,0:T(2,128)(2,1)} %param.5) | data formatting | bytes 9830400 | tf_op jit(solution)/shard_map/reshape | solution.py:276
  12.2 50.3 %collective-permute-done = bf16[150,2,4096]{2,1,0:T(2,128)(2,1)} collective-permute-done((bf16[150,2,4096]{2,1,0:T(2,128)(2,1)S(1)}, bf16[150,2,4096]{2,1,0:T(2,128)(2,1)}, u32[]{:S(2)}, u32[]{:S(2)}) %collective-permute-start) | collective-permute-done | bytes 2457632 | tf_op jit(solution)/shard_map/ppermute | solution.py:25
  62.5 4.2 %broadcast_select_fusion = bf16[150,2,4096]{2,1,0:T(2,128)(2,1)S(1)} fusion(bf16[150,2,4096]{2,1,0:T(2,128)(2,1)} %param.6, bf16[150,2,4096]{2,1,0:T(2,128)(2,1)} %collective-permute-done, pred[]{:T(512)S(6)} %eq.3), kind=kLoop, calls=%fused_computation | loop fusion | flops 1228800 | bytes 7372801 | tf_op jit(solution)/shard_map/jit(_where)/select_n | solution.py:275
  66.7 2.5 %pad = bf16[152,2,4096]{2,1,0:T(2,128)(2,1)S(1)} pad(bf16[150,2,4096]{2,1,0:T(2,128)(2,1)S(1)} %broadcast_select_fusion, bf16[]{:T(256)} %constant.6), padding=0_2x0_0x0_0 | pad | bytes 4947970
  69.3 3.1 %copy.9 = bf16[19,8,2,4096]{3,1,2,0:T(8,128)(2,1)} copy(bf16[19,8,2,4096]{3,2,1,0:T(2,128)(2,1)S(1)} %bitcast.6) | data formatting | bytes 4980736
  72.3 8.9 %gram.1.x_ref = f32[1024,128]{1,0:T(8,128)} custom-call(bf16[2,150,8192]{2,1,0:T(8,128)(2,1)} %reshape.10.own_ref.refs_0_.refs_1_, bf16[150,8192]{1,0:T(8,128)(2,1)} %bitcast.3), custom_call_target="tpu_custom_call" | custom-call | tf_op jit(solution)/shard_map/gram/pallas_call | solution.py:64
  81.2 30.1 %sum_over_pix.1.packed_ref = f32[1024,128]{1,0:T(8,128)} custom-call(f32[1024,128]{1,0:T(8,128)} %gram.1.x_ref), custom_call_target="tpu_custom_call" | custom-call | tf_op jit(solution)/shard_map/sum_over_pix/pallas_call | solution.py:131
  111.3 43.2 %iterate.1 = (f32[2,300,128]{2,1,0:T(8,128)}, bf16[2,2,2,150,150]{4,3,2,1,0:T(8,128)(2,1)}) custom-call(s32[2]{0:T(128)} %low_ref.1, s32[2]{0:T(128)} %high_ref.1, f32[1024,128]{1,0:T(8,128)} %sum_over_pix.1.packed_ref, f32[300,128]{1,0:T(8,128)} %start_ref.1), custom_call_target="tpu_custom_call" | custom-call | tf_op jit(solution)/shard_map/iterate/pallas_call | solution.py:220
  154.5 0.0 copy-start
  154.5 10.0 %filter.1 = f32[2,4096]{1,0:T(2,128)} custom-call(bf16[2,2,2,150,150]{4,3,2,1,0:T(8,128)(2,1)} %get-tuple-element.4.proj_ref, bf16[2,150,8192]{2,1,0:T(8,128)(2,1)} %reshape.10.own_ref.refs_0_.refs_1_, bf16[2,150,8192]{2,1,0:T(8,128)(2,1)} %reshape.10.own_ref.refs_0_.refs_1_, bf16[150,8192]{1,0:T(8,128)(2,1)} %bitcast.4, bf16[150,8192]{1,0:T(8,128)(2,1)} %bitcast.5), custom_call_target="tpu_custom_call" | custom-call | tf_op jit(solution)/shard_map/filter/pallas_call | solution.py:255
  164.5 0.0 copy-done
  164.5 0.9 copy.8
Async XLA Ops:
  4.7 57.8 %collective-permute-start = (bf16[150,2,4096]{2,1,0:T(2,128)(2,1)S(1)}, bf16[150,2,4096]{2,1,0:T(2,128)(2,1)}, u32[]{:S(2)}, u32[]{:S(2)}) collective-permute-start(bf16[150,2,4096]{2,1,0:T(2,128)(2,1)S(1)} %slice.3), channel_id=1, source_target_pairs={{1,0},{3,2},{5,4},{7,6},{9,8},{11,10},{13,12},{15,14},{17,16},{19,... | collective-permute-start | bytes 7372808 | tf_op jit(solution)/shard_map/ppermute | solution.py:25
  154.5 10.1 %copy-start = (f32[2,300,128]{2,1,0:T(8,128)S(1)}, f32[2,300,128]{2,1,0:T(8,128)}, u32[]{:S(2)}) copy-start(f32[2,300,128]{2,1,0:T(8,128)} %get-tuple-element.9) | copy-start | bytes 921604

commit v3 on v2

--- a/solution.py
+++ b/solution.py
@@ -17,12 +17,6 @@
 MESH = pl.DeviceIdType.MESH
 VMEM = pl.BlockSpec(memory_space=pltpu.VMEM)
 SMEM = pl.BlockSpec(memory_space=pltpu.SMEM)
-
-
-def from_behind(block, axis, distance):
-    devices = range(lax.axis_size(axis))
-    route = [(i - distance, i) for i in devices if i - distance in devices]
-    return lax.ppermute(block, axis, route)
 
 
 def dot(a, b, ca, cb, precision=HI):
@@ -75,8 +69,64 @@
     )(own, following)
 
 
-def sum_kernel(n, x_ref, out_ref, acc, landed, gathered, send_sem, recv_sem):
+def cross_kernel(half, place_ref, own_ref, swapped_ref, packed_ref, extra_ref, acc):
+    step = pl.program_id(0)
+
+    @pl.when(step == 0)
+    def _():
+        acc[...] = jnp.zeros_like(acc)
+
+    front = place_ref[0] == 0
+    mine, theirs = own_ref[0], swapped_ref[...]
+    acc[...] += dot(
+        jnp.where(front, mine, theirs), jnp.where(front, theirs, mine), 1, 1, None
+    )
+
+    @pl.when(step == pl.num_programs(0) - 1)
+    def _():
+        pitch = up(half, SUB)
+        rest = half - LANES
+        extra_ref[...] = jnp.zeros_like(extra_ref)
+        extra_ref[:half] = acc[:, :LANES]
+        extra_ref[pitch : pitch + half] = packed_ref[:half]
+        extra_ref[2 * pitch : 2 * pitch + half] = jnp.concatenate(
+            [
+                jnp.zeros((half, 3 * rest), jnp.float32),
+                acc[:, LANES:],
+                packed_ref[pitch * BLOCKS : pitch * BLOCKS + half, :rest],
+                jnp.zeros((half, LANES - BLOCKS * rest), jnp.float32),
+            ],
+            axis=1,
+        )
+
+
+def cross_block(place, own, swapped, packed):
+    _, half, columns = own.shape
+    tile = 1024
+    count = columns // 2 // tile
+    rows = 3 * up(half, SUB)
+    return pl.pallas_call(
+        functools.partial(cross_kernel, half),
+        out_shape=jax.ShapeDtypeStruct((rows, LANES), jnp.float32),
+        grid_spec=pltpu.PrefetchScalarGridSpec(
+            num_scalar_prefetch=1,
+            grid=(count,),
+            in_specs=[
+                pl.BlockSpec((1, half, tile), lambda i, t: (1 - t[0], 0, i + t[0] * count)),
+                pl.BlockSpec((half, tile), lambda i, t: (0, i)),
+                pl.BlockSpec(packed.shape, lambda i, t: (0, 0)),
+            ],
+            out_specs=pl.BlockSpec((rows, LANES), lambda i, t: (0, 0)),
+            scratch_shapes=[pltpu.VMEM((half, half), jnp.float32)],
+        ),
+        name="cross",
+    )(place, own, swapped, packed)
+
+
+def sum_kernel(n, extra, x_ref, extra_ref, out_ref, whole, arrived, acc, landed, gathered, send_sem, recv_sem):
     me = lax.axis_index("pix")
+    front = lax.axis_index("tm") == 0
+    other = 1 - lax.axis_index("tm")
     bits = n.bit_length() - 1
     bit = [lax.rem(me // (1 << b), 2) for b in range(bits)]
     partner = [me + (1 - 2 * bit[b]) * (1 << b) for b in range(bits)]
@@ -86,7 +136,33 @@
         pl.semaphore_signal(
             barrier, inc=1, device_id={"pix": partner[b]}, device_id_type=MESH
         )
-    pl.semaphore_wait(barrier, bits)
+    pl.semaphore_signal(barrier, inc=1, device_id={"tm": other}, device_id_type=MESH)
+    pl.semaphore_wait(barrier, bits + 1)
+
+    copy = pltpu.make_async_remote_copy(
+        src_ref=extra_ref,
+        dst_ref=arrived,
+        send_sem=send_sem.at[2 * bits],
+        recv_sem=recv_sem.at[2 * bits],
+        device_id={"tm": other},
+        device_id_type=MESH,
+    )
+    copy.start()
+    pitch = extra_ref.shape[0] // 3
+    cross, low, rest = pl.ds(0, pitch), pl.ds(pitch, pitch), pl.ds(2 * pitch, pitch)
+    whole[pl.ds(0, 3 * pitch)] = x_ref[pl.ds(0, 3 * pitch)]
+    tail = 6 * pitch
+    whole[pl.ds(tail, x_ref.shape[0] - tail)] = x_ref[pl.ds(tail, x_ref.shape[0] - tail)]
+    copy.wait()
+    at = pl.ds(3 * pitch, pitch)
+    whole[at] = jnp.where(front, extra_ref[cross] + arrived[cross], x_ref[at])
+    at = pl.ds(4 * pitch, pitch)
+    whole[at] = jnp.where(front, arrived[low], x_ref[at])
+    at = pl.ds(5 * pitch, pitch)
+    lane = lax.broadcasted_iota(jnp.int32, (pitch, LANES), 1)
+    merged = jnp.where(lane < 3 * extra, x_ref[at], arrived[rest])
+    merged += jnp.where((lane >= 3 * extra) & (lane < 4 * extra), extra_ref[rest], 0.0)
+    whole[at] = jnp.where(front, merged, x_ref[at])
 
     def window(start, size):
         return pl.ds(pl.multiple_of(start, SUB), size)
@@ -96,7 +172,7 @@
         size //= 2
         keep = start + bit[b] * size
         give = start + (1 - bit[b]) * size
-        source = x_ref if b == 0 else acc
+        source = whole if b == 0 else acc
         copy = pltpu.make_async_remote_copy(
             src_ref=source.at[window(give, size)],
             dst_ref=landed.at[pl.ds(base, size)],
@@ -125,24 +201,26 @@
     out_ref[...] = gathered[...]
 
 
-def sum_over_pix(packed):
+def sum_over_pix(packed, crossing, half):
     n = lax.axis_size("pix")
     bits = n.bit_length() - 1
     return pl.pallas_call(
-        functools.partial(sum_kernel, n),
+        functools.partial(sum_kernel, n, half - LANES),
         out_shape=jax.ShapeDtypeStruct(packed.shape, jnp.float32),
-        in_specs=[VMEM],
+        in_specs=[VMEM, VMEM],
         out_specs=VMEM,
         scratch_shapes=[
             pltpu.VMEM(packed.shape, jnp.float32),
+            pltpu.VMEM(crossing.shape, jnp.float32),
             pltpu.VMEM(packed.shape, jnp.float32),
             pltpu.VMEM(packed.shape, jnp.float32),
-            pltpu.SemaphoreType.DMA((2 * bits,)),
-            pltpu.SemaphoreType.DMA((2 * bits,)),
+            pltpu.VMEM(packed.shape, jnp.float32),
+            pltpu.SemaphoreType.DMA((2 * bits + 1,)),
+            pltpu.SemaphoreType.DMA((2 * bits + 1,)),
         ],
         compiler_params=pltpu.CompilerParams(collective_id=0, has_side_effects=True),
         name="sum_over_pix",
-    )(packed)
+    )(packed, crossing)
 
 
 def inverse_factors(grams):
@@ -229,17 +307,22 @@
             pltpu.VMEM((BLOCKS, half, half), jnp.float32),
             pltpu.VMEM((WIN_DEV, 2, half, K), jnp.float32),
         ],
+        cost_estimate=pl.CostEstimate(flops=40_000_000_000, bytes_accessed=1_000_000, transcendentals=0),
         name="iterate",
     )(low, high, packed, start)
 
 
-def filter_kernel(half, proj_ref, *refs):
-    own, following, power_ref = refs[:2], refs[2:4], refs[4]
+def filter_kernel(half, place_ref, proj_ref, *refs):
+    own, arrived, tail, power_ref = refs[:2], refs[2:4], refs[4:6], refs[6]
+    front = place_ref[0] == 0
     for w in range(WIN_DEV):
         total = 0.0
         for part in range(2):
             above = own[part][w]
-            below = own[part][1] if w == 0 else following[part][...]
+            if w == 0:
+                below = own[part][1]
+            else:
+                below = jnp.where(front, arrived[part][...], tail[part][...])
             for i in range(2):
                 rows = dot(proj_ref[w, i, 0], above, 1, 0, None)
                 rows += dot(proj_ref[w, i, 1], below, 1, 0, None)
@@ -247,7 +330,7 @@
         power_ref[w : w + 1] = total / (2 * half)
 
 
-def filtered_power(projs, own, following):
+def filtered_power(place, projs, own, arrived, tail):
     _, half, columns = own.shape
     pixels = columns // 2
     tile = 512
@@ -257,27 +340,39 @@
         out_shape=jax.ShapeDtypeStruct((WIN_DEV, pixels), jnp.float32),
         grid=(count,),
         in_specs=[
+            SMEM,
             pl.BlockSpec(projs.shape, lambda i: (0, 0, 0, 0, 0)),
             pl.BlockSpec((2, half, tile), lambda i: (0, 0, i)),
             pl.BlockSpec((2, half, tile), lambda i: (0, 0, i + count)),
+            pl.BlockSpec((half, tile), lambda i: (0, i)),
+            pl.BlockSpec((half, tile), lambda i: (0, i)),
             pl.BlockSpec((half, tile), lambda i: (0, i)),
             pl.BlockSpec((half, tile), lambda i: (0, i + count)),
         ],
         out_specs=pl.BlockSpec((WIN_DEV, tile), lambda i: (0, i)),
         name="filter",
-    )(projs, own, own, following, following)
+    )(place, projs, own, own, *arrived, tail, tail)
 
 
 def body(iq, tail_frames, start_basis, low_rank, high_rank):
+    assert lax.axis_size("tm") == 2
     half = iq.shape[0] // WIN_DEV
-    incoming = from_behind(iq[:half], "tm", -1)
-    at_end = lax.axis_index("tm") == lax.axis_size("tm") - 1
-    following = jnp.where(at_end, tail_frames, incoming).reshape(half, -1)
+    place = lax.axis_index("tm")
+    front = place == 0
+    place = place.reshape(1).astype(jnp.int32)
+    swapped = lax.ppermute(
+        jnp.where(front, iq[half:, 1], iq[:half, 0]), "tm", [(0, 1), (1, 0)]
+    )
     own = iq.reshape(WIN_DEV, half, -1)
+    tail = tail_frames.reshape(half, -1)
     rows = up(up(half, SUB) * (BLOCKS + 1), SUB * lax.axis_size("pix"))
-    packed = sum_over_pix(gram_blocks(own, following, rows))
-    bases, projs = iterate(packed, start_basis, low_rank, high_rank)
-    return (filtered_power(projs, own, following), bases)
+    packed = gram_blocks(own, tail, rows)
+    crossing = cross_block(place, own, swapped, packed)
+    summed = sum_over_pix(packed, crossing, half)
+    late, summed = lax.optimization_barrier((iq[:half, 1], summed))
+    late = lax.ppermute(late, "tm", [(1, 0)])
+    bases, projs = iterate(summed, start_basis, low_rank, high_rank)
+    return (filtered_power(place, projs, own, (swapped, late), tail), bases)
 
 
 def solution(mesh):

time: 166 us -> 149 us (0.90)
  waiting for transfers between devices: 50.3 us -> 3.45 us
  local copies, waits for them, and re-layouts: 16.7 us -> 32.3 us
  Pallas kernels: 92.2 us -> 102 us
  starting transfers between devices: 1.29 us -> 4.26 us
    ppermute x1 -> x2, waiting for transfers between devices: 50.3 us -> 3.45 us  [the longest x1 3.44 us: body(): lax.ppermute(jnp.where(front, iq[half:, 1], iq[:half, 0]), 'tm', [(0, 1),...]
    pallas_call x1 -> x2, Pallas kernels: 30.1 us -> 39.6 us  [the longest x1 35.6 us: sum_over_pix(): pl.pallas_call(functools.partial(sum_kernel, n, half - LANES), out_shape=...]
    slice x1, local copies, waits for them, and re-layouts: 4.1 us -> 13.2 us  [body(): iq[half:, 1]]
    unnamed x5 -> x10, local copies, waits for them, and re-layouts: 6.48 us -> 12.9 us
    ppermute x1 -> x2, starting transfers between devices: 1.29 us -> 4.26 us  [the longest x1 2.97 us: body(): lax.ppermute(jnp.where(front, iq[half:, 1], iq[:half, 0]), 'tm', [(0, 1),...]
  transfers between devices with their start and end apart: 1 -> 2, of which waited for: 1 -> 1; matrix products, arithmetic and copies ran while one was open for 4% -> 11% of each run, Pallas kernels for 0% -> 35%
where the time goes in v3:
time: 149 us; the launch traced here: 148 us
  Pallas kernels  102 us (68%)
  local copies, waits for them, and re-layouts  32.3 us (22%)
  other arithmetic  5.34 us (4%)
  starting transfers between devices  4.26 us (3%)
  waiting for transfers between devices  3.45 us (2%)
    pallas_call x1, Pallas kernels, iterate(): pl.pallas_call(functools.partial(iterate_kernel, half), out_shape=(jax.Sh...  43 us
    pallas_call x1, Pallas kernels, sum_over_pix(): pl.pallas_call(functools.partial(sum_kernel, n, half - LANES), out_shape=...  35.6 us
    slice x1, local copies, waits for them, and re-layouts, body(): iq[half:, 1]  13.2 us
    unnamed x10, local copies, waits for them, and re-layouts  12.9 us
    pallas_call x1, Pallas kernels, filtered_power(): pl.pallas_call(functools.partial(filter_kernel, half), out_shape=jax.Shap...  10.5 us
    pallas_call x1, Pallas kernels, gram_blocks(): pl.pallas_call(functools.partial(gram_kernel, half), out_shape=jax.ShapeD...  9.14 us
    reshape x1, local copies, waits for them, and re-layouts, body(): own = iq.reshape(WIN_DEV, half, -1)  6.19 us
    select_n x1, other arithmetic, body(): jnp.where(front, iq[half:, 1], iq[:half, 0])  5.34 us
  transfers between devices with their start and end apart: 2, of which 1 were waited for; matrix products, arithmetic and copies ran while one was open for 11% of the time, Pallas kernels for 35%

profile of v3, /device:TPU:0, one launch (start us, length us, event | category | flops | bytes accessed | tf_op | source)
XLA Modules:
  0.0 148.3 jit_solution(16049455738234129786)
XLA Ops:
  0.6 13.2 %fusion.1 = (bf16[150,1,4096]{2,1,0:T(2,128)(2,1)S(1)}, bf16[150,1,4096]{2,1,0:T(2,128)(2,1)}, bf16[150,1,4096]{2,1,0:T(2,128)(2,1)}) fusion(bf16[300,2,4096]{2,1,0:T(2,128)(2,1)} %param.5), kind=kLoop, calls=%fused_computation.3 | loop fusion | bytes 7372800 | tf_op jit(solution)/shard_map/slice | solution.py:364
  13.8 5.3 %fusion = bf16[150,4096]{1,0:T(8,128)(2,1)} fusion(bf16[150,1,4096]{2,1,0:T(2,128)(2,1)} %get-tuple-element.16, bf16[150,1,4096]{2,1,0:T(2,128)(2,1)S(1)} %get-tuple-element.14, pred[]{:T(512)S(6)} %eq.3), kind=kLoop, calls=%fused_computation.1 | loop fusion | flops 614400 | bytes 3686401 | tf_op jit(solution)/shard_map/jit(_where)/select_n | solution.py:364
  19.2 3.0 %collective-permute-start = (bf16[150,4096]{1,0:T(8,128)(2,1)}, bf16[150,4096]{1,0:T(8,128)(2,1)S(1)}, u32[]{:S(2)}, u32[]{:S(2)}) collective-permute-start(bf16[150,4096]{1,0:T(8,128)(2,1)} %fusion), channel_id=1, source_target_pairs={{0,1},{1,0},{2,3},{3,2},{4,5},{5,4},{6,7},{7,6},{8,9},{9,8},{10,11... | collective-permute-start | bytes 3686408 | tf_op jit(solution)/shard_map/ppermute | solution.py:363
  22.1 6.2 %reshape.16.own_ref.refs_0_.refs_1_ = bf16[2,150,8192]{2,1,0:T(8,128)(2,1)} reshape(bf16[300,2,4096]{2,1,0:T(2,128)(2,1)} %param.5) | data formatting | bytes 9830400 | tf_op jit(solution)/shard_map/reshape | solution.py:366
  28.3 4.3 %pad = bf16[152,2,4096]{2,1,0:T(2,128)(2,1)S(1)} pad(bf16[150,2,4096]{2,1,0:T(2,128)(2,1)} %param.6, bf16[]{:T(256)} %constant.6), padding=0_2x0_0x0_0 | pad | bytes 4947970
  32.7 0.0 copy-start
  32.7 3.1 %copy.18 = bf16[19,8,2,4096]{3,1,2,0:T(8,128)(2,1)} copy(bf16[19,8,2,4096]{3,2,1,0:T(2,128)(2,1)S(1)} %bitcast.12) | data formatting | bytes 4980736
  35.8 0.0 copy-done
  35.8 1.3 copy.24
  37.1 9.1 %gram.1.packed_ref.x_ref = f32[1024,128]{1,0:T(8,128)} custom-call(bf16[2,150,8192]{2,1,0:T(8,128)(2,1)} %reshape.16.own_ref.refs_0_.refs_1_, bf16[150,8192]{1,0:T(8,128)(2,1)} %bitcast.9), custom_call_target="tpu_custom_call" | custom-call | tf_op jit(solution)/shard_map/gram/pallas_call | solution.py:58
  46.3 3.4 %collective-permute-done.swapped_ref.refs_2_ = bf16[150,4096]{1,0:T(8,128)(2,1)S(1)} collective-permute-done((bf16[150,4096]{1,0:T(8,128)(2,1)}, bf16[150,4096]{1,0:T(8,128)(2,1)S(1)}, u32[]{:S(2)}, u32[]{:S(2)}) %collective-permute-start) | collective-permute-done | bytes 1228832 | tf_op jit(solution)/shard_map/ppermute | solution.py:363
  49.7 0.0 copy-start.1
  49.7 1.1 copy-done.1
  50.9 4.0 %cross.1.extra_ref = f32[456,128]{1,0:T(8,128)} custom-call(s32[1]{0:T(128)} %bitcast.place_ref, bf16[2,150,8192]{2,1,0:T(8,128)(2,1)} %reshape.16.own_ref.refs_0_.refs_1_, bf16[150,4096]{1,0:T(8,128)(2,1)} %copy-done.1, f32[1024,128]{1,0:T(8,128)} %gram.1.packed_ref.x_ref), custom_call_target="tpu_custom_call" | custom-call | tf_op jit(solution)/shard_map/cross/pallas_call | solution.py:108
  54.9 35.6 %sum_over_pix.1.packed_ref = f32[1024,128]{1,0:T(8,128)} custom-call(f32[1024,128]{1,0:T(8,128)} %gram.1.packed_ref.x_ref, f32[456,128]{1,0:T(8,128)} %cross.1.extra_ref), custom_call_target="tpu_custom_call" | custom-call | tf_op jit(solution)/shard_map/sum_over_pix/pallas_call | solution.py:207
  90.5 1.3 collective-permute-start.1
  91.8 43.0 %iterate.1 = (f32[2,300,128]{2,1,0:T(8,128)}, bf16[2,2,2,150,150]{4,3,2,1,0:T(8,128)(2,1)}) custom-call(s32[2]{0:T(128)} %low_ref.1, s32[2]{0:T(128)} %high_ref.1, f32[1024,128]{1,0:T(8,128)} %sum_over_pix.1.packed_ref, f32[300,128]{1,0:T(8,128)} %start_ref.1), custom_call_target="tpu_custom_call" | custom-call | flops 40000000000 | bytes 1000000 | tf_op jit(solution)/shard_map/iterate/pallas_call | solution.py:298
  134.8 1.8 %copy.14 = f32[2,300,128]{2,0,1:T(2,128)} copy(f32[2,300,128]{2,1,0:T(8,128)} %get-tuple-element.13) | data formatting | bytes 614400
  136.6 0.0 collective-permute-done.1.refs_3_
  136.6 0.0 copy-start.2
  136.6 1.1 copy-done.2
  137.8 10.5 %filter.1 = f32[2,4096]{1,0:T(2,128)} custom-call(s32[1]{0:T(128)} %bitcast.place_ref, bf16[2,2,2,150,150]{4,3,2,1,0:T(8,128)(2,1)} %get-tuple-element.7.proj_ref, bf16[2,150,8192]{2,1,0:T(8,128)(2,1)} %reshape.16.own_ref.refs_0_.refs_1_, bf16[2,150,8192]{2,1,0:T(8,128)(2,1)} %reshape.16.own_ref.refs_0_.refs_1_, bf16[150,4096]{1,0:T(8,128)(2,1)} %copy-done.1, ...), custom_call_target="tpu_custom_call" | custom-call | tf_op jit(solution)/shard_map/filter/pallas_call | solution.py:338
Async XLA Ops:
  19.2 30.5 %collective-permute-start = (bf16[150,4096]{1,0:T(8,128)(2,1)}, bf16[150,4096]{1,0:T(8,128)(2,1)S(1)}, u32[]{:S(2)}, u32[]{:S(2)}) collective-permute-start(bf16[150,4096]{1,0:T(8,128)(2,1)} %fusion), channel_id=1, source_target_pairs={{0,1},{1,0},{2,3},{3,2},{4,5},{5,4},{6,7},{7,6},{8,9},{9,8},{10,11... | collective-permute-start | bytes 3686408 | tf_op jit(solution)/shard_map/ppermute | solution.py:363
  32.7 3.1 %copy-start = (bf16[150,1,4096]{2,1,0:T(2,128)(2,1)S(1)}, bf16[150,1,4096]{2,1,0:T(2,128)(2,1)}, u32[]{:S(2)}) copy-start(bf16[150,1,4096]{2,1,0:T(2,128)(2,1)} %get-tuple-element.15) | copy-start | bytes 3686404
  49.7 1.1 copy-start.1
  90.5 46.1 %collective-permute-start.1 = (bf16[150,4096]{1,0:T(8,128)(2,1)S(1)}, bf16[150,4096]{1,0:T(8,128)(2,1)S(1)}, u32[]{:S(2)}, u32[]{:S(2)}) collective-permute-start(bf16[150,4096]{1,0:T(8,128)(2,1)S(1)} %bitcast.13), channel_id=1, source_target_pairs={{1,0},{3,2},{5,4},{7,6},{9,8},{11,10},{13,12},{15,14},{17,16},{19,... | collective-permute-start | bytes 3686408 | tf_op jit(solution)/shard_map/ppermute | solution.py:373
  136.6 1.1 copy-start.2

commit v4 on v3

--- a/solution.py
+++ b/solution.py
@@ -11,6 +11,7 @@
 ITERS = 3
 WIN_DEV = 2
 SUB = 8
+PANEL = 4
 LANES = 128
 BLOCKS = 5
 HI = lax.Precision.HIGHEST
@@ -228,18 +229,31 @@
     lane = lax.broadcasted_iota(jnp.int32, (SUB, K), 1)
     sub = lax.broadcasted_iota(jnp.int32, (SUB, K), 0)
     work = [[m[SUB * u : SUB * u + SUB, :] for u in range(tiles)] for m in grams]
-    for j in range(K):
-        t, s = divmod(j, SUB)
-        here = lane == j
+    for start in range(0, K, PANEL):
+        t = start // SUB
         for rows in work:
-            pivot = rows[t][s : s + 1, j : j + 1]
-            scaled = jnp.where(here[:1], 1.0, rows[t][s : s + 1, :]) * (1.0 / pivot)
-            for u in range(t, tiles):
-                if u == t and s == SUB - 1:
-                    continue
-                column = rows[u][:, j : j + 1]
-                update = jnp.where(here, 0.0, rows[u]) - column * scaled
-                rows[u] = jnp.where(sub > s, update, rows[u]) if u == t else update
+            spread = [
+                {
+                    u: jnp.broadcast_to(rows[u][:, start + p : start + p + 1], (SUB, K))
+                    for u in range(t, tiles)
+                }
+                for p in range(PANEL)
+            ]
+            for p in range(PANEL):
+                s = (start + p) % SUB
+                here = lane == start + p
+                inverse = 1.0 / spread[p][t][s : s + 1, :]
+                scaled = jnp.where(here[:1], 1.0, rows[t][s : s + 1, :]) * inverse
+                factors = [spread[q][t][s : s + 1, :] * inverse for q in range(p + 1, PANEL)]
+                for u in range(t, tiles):
+                    if u == t and s == SUB - 1:
+                        continue
+                    column = spread[p][u]
+                    for q, factor in zip(range(p + 1, PANEL), factors):
+                        update = spread[q][u] - column * factor
+                        spread[q][u] = jnp.where(sub > s, update, spread[q][u]) if u == t else update
+                    update = jnp.where(here, 0.0, rows[u]) - column * scaled
+                    rows[u] = jnp.where(sub > s, update, rows[u]) if u == t else update
     inverses = []
     for rows in work:
         out = []
@@ -360,16 +374,17 @@
     place = lax.axis_index("tm")
     front = place == 0
     place = place.reshape(1).astype(jnp.int32)
+    own = iq.reshape(WIN_DEV, half, -1)
+    middle = own.shape[2] // 2
     swapped = lax.ppermute(
-        jnp.where(front, iq[half:, 1], iq[:half, 0]), "tm", [(0, 1), (1, 0)]
+        jnp.where(front, own[1, :, middle:], own[0, :, :middle]), "tm", [(0, 1), (1, 0)]
     )
-    own = iq.reshape(WIN_DEV, half, -1)
     tail = tail_frames.reshape(half, -1)
     rows = up(up(half, SUB) * (BLOCKS + 1), SUB * lax.axis_size("pix"))
     packed = gram_blocks(own, tail, rows)
     crossing = cross_block(place, own, swapped, packed)
     summed = sum_over_pix(packed, crossing, half)
-    late, summed = lax.optimization_barrier((iq[:half, 1], summed))
+    late, summed = lax.optimization_barrier((own[0, :, middle:], summed))
     late = lax.ppermute(late, "tm", [(1, 0)])
     bases, projs = iterate(summed, start_basis, low_rank, high_rank)
     return (filtered_power(place, projs, own, (swapped, late), tail), bases)

time: 149 us -> 126 us (0.85)
  local copies, waits for them, and re-layouts: 32.3 us -> 16 us
  Pallas kernels: 102 us -> 86.7 us
  waiting for transfers between devices: 3.45 us -> 13.6 us
  other arithmetic: 5.34 us -> 3.55 us
    pallas_call x1, Pallas kernels: 43 us -> 27.5 us  [iterate(): pl.pallas_call(functools.partial(iterate_kernel, half), out_shape=(jax.Sh...]
    slice x1 -> x0, local copies, waits for them, and re-layouts: 13.2 us -> none  [body(): iq[half:, 1]]
    ppermute x1, waiting for transfers between devices: 3.44 us -> 12.9 us  [body(): lax.ppermute(jnp.where(front, own[1, :, middle:], own[0, :, :middle]), 't...]
    unnamed x10 -> x9, local copies, waits for them, and re-layouts: 12.9 us -> 9.82 us
    select_n x1, other arithmetic: 5.34 us -> 3.55 us  [body(): jnp.where(front, own[1, :, middle:], own[0, :, :middle])]
  transfers between devices with their start and end apart: 2 -> 2, of which waited for: 1 -> 2; matrix products, arithmetic and copies ran while one was open for 11% -> 6% of each run, Pallas kernels for 35% -> 29%
where the time goes in v4:
time: 126 us; the launch traced here: 125 us
  Pallas kernels  86.7 us (69%)
  local copies, waits for them, and re-layouts  16 us (13%)
  waiting for transfers between devices  13.6 us (11%)
  starting transfers between devices  4.44 us (4%)
  other arithmetic  3.55 us (3%)
    pallas_call x1, Pallas kernels, sum_over_pix(): pl.pallas_call(functools.partial(sum_kernel, n, half - LANES), out_shape=...  35.6 us
    pallas_call x1, Pallas kernels, iterate(): pl.pallas_call(functools.partial(iterate_kernel, half), out_shape=(jax.Sh...  27.5 us
    ppermute x1, waiting for transfers between devices, body(): lax.ppermute(jnp.where(front, own[1, :, middle:], own[0, :, :middle]), 't...  12.9 us
    pallas_call x1, Pallas kernels, filtered_power(): pl.pallas_call(functools.partial(filter_kernel, half), out_shape=jax.Shap...  10.5 us
    unnamed x9, local copies, waits for them, and re-layouts  9.82 us
    pallas_call x1, Pallas kernels, gram_blocks(): pl.pallas_call(functools.partial(gram_kernel, half), out_shape=jax.ShapeD...  8.95 us
    reshape x1, local copies, waits for them, and re-layouts, body(): own = iq.reshape(WIN_DEV, half, -1)  6.19 us
    pallas_call x1, Pallas kernels, cross_block(): pl.pallas_call(functools.partial(cross_kernel, half), out_shape=jax.Shape...  4.01 us
  transfers between devices with their start and end apart: 2, of which 2 were waited for; matrix products, arithmetic and copies ran while one was open for 6% of the time, Pallas kernels for 29%

profile of v4, /device:TPU:0, one launch (start us, length us, event | category | flops | bytes accessed | tf_op | source)
XLA Modules:
  0.0 124.9 jit_solution(14032424901243120235)
XLA Ops:
  0.6 6.2 %reshape.16.own_ref.refs_0_.refs_1_ = bf16[2,150,8192]{2,1,0:T(8,128)(2,1)} reshape(bf16[300,2,4096]{2,1,0:T(2,128)(2,1)} %param.5) | data formatting | bytes 9830400 | tf_op jit(solution)/shard_map/reshape | solution.py:377
  6.8 0.0 copy-start.1
  6.8 3.5 %fusion = (bf16[150,4096]{1,0:T(8,128)(2,1)}, bf16[150,4096]{1,0:T(8,128)(2,1)S(1)}) fusion(bf16[2,150,8192]{2,1,0:T(8,128)(2,1)} %reshape.16.own_ref.refs_0_.refs_1_, pred[]{:T(512)S(6)} %eq.3), kind=kLoop, calls=%fused_computation.1 | loop fusion | flops 614400 | bytes 6144001 | tf_op jit(solution)/shard_map/jit(_where)/select_n | solution.py:380
  10.4 3.0 %collective-permute-start = (bf16[150,4096]{1,0:T(8,128)(2,1)}, bf16[150,4096]{1,0:T(8,128)(2,1)S(1)}, u32[]{:S(2)}, u32[]{:S(2)}) collective-permute-start(bf16[150,4096]{1,0:T(8,128)(2,1)} %get-tuple-element.14), channel_id=1, source_target_pairs={{0,1},{1,0},{2,3},{3,2},{4,5},{5,4},{6,7},{7,6},{8,9},{9,8},{10,11... | collective-permute-start | bytes 3686408 | tf_op jit(solution)/shard_map/ppermute | solution.py:379
  13.3 0.0 copy-done.1
  13.3 2.6 %pad = bf16[152,2,4096]{2,1,0:T(2,128)(2,1)S(1)} pad(bf16[150,2,4096]{2,1,0:T(2,128)(2,1)S(1)} %copy-done.1, bf16[]{:T(256)} %constant.6), padding=0_2x0_0x0_0 | pad | bytes 4947970
  16.0 3.1 %copy.9 = bf16[19,8,2,4096]{3,1,2,0:T(8,128)(2,1)} copy(bf16[19,8,2,4096]{3,2,1,0:T(2,128)(2,1)S(1)} %bitcast.11) | data formatting | bytes 4980736
  19.1 9.0 %gram.1.packed_ref.x_ref = f32[1024,128]{1,0:T(8,128)} custom-call(bf16[2,150,8192]{2,1,0:T(8,128)(2,1)} %reshape.16.own_ref.refs_0_.refs_1_, bf16[150,8192]{1,0:T(8,128)(2,1)} %bitcast.8), custom_call_target="tpu_custom_call" | custom-call | tf_op jit(solution)/shard_map/gram/pallas_call | solution.py:59
  28.0 12.9 %collective-permute-done.swapped_ref.refs_2_ = bf16[150,4096]{1,0:T(8,128)(2,1)S(1)} collective-permute-done((bf16[150,4096]{1,0:T(8,128)(2,1)}, bf16[150,4096]{1,0:T(8,128)(2,1)S(1)}, u32[]{:S(2)}, u32[]{:S(2)}) %collective-permute-start) | collective-permute-done | bytes 1228832 | tf_op jit(solution)/shard_map/ppermute | solution.py:379
  40.9 0.0 copy-start
  40.9 1.1 copy-done
  42.1 4.0 %cross.1.extra_ref = f32[456,128]{1,0:T(8,128)} custom-call(s32[1]{0:T(128)} %bitcast.place_ref, bf16[2,150,8192]{2,1,0:T(8,128)(2,1)} %reshape.16.own_ref.refs_0_.refs_1_, bf16[150,4096]{1,0:T(8,128)(2,1)} %copy-done, f32[1024,128]{1,0:T(8,128)} %gram.1.packed_ref.x_ref), custom_call_target="tpu_custom_call" | custom-call | tf_op jit(solution)/shard_map/cross/pallas_call | solution.py:109
  46.1 35.6 %sum_over_pix.1.packed_ref = f32[1024,128]{1,0:T(8,128)} custom-call(f32[1024,128]{1,0:T(8,128)} %gram.1.packed_ref.x_ref, f32[456,128]{1,0:T(8,128)} %cross.1.extra_ref), custom_call_target="tpu_custom_call" | custom-call | tf_op jit(solution)/shard_map/sum_over_pix/pallas_call | solution.py:208
  81.7 1.5 %collective-permute-start.1 = (bf16[150,4096]{1,0:T(8,128)(2,1)S(1)}, bf16[150,4096]{1,0:T(8,128)(2,1)S(1)}, u32[]{:S(2)}, u32[]{:S(2)}) collective-permute-start(bf16[150,4096]{1,0:T(8,128)(2,1)S(1)} %get-tuple-element.8), channel_id=1, source_target_pairs={{1,0},{3,2},{5,4},{7,6},{9,8},{11,10},{13,12},{15,14},{17,16},{19,... | collective-permute-start | bytes 3686408 | tf_op jit(solution)/shard_map/ppermute | solution.py:388
  83.2 27.5 %iterate.1 = (f32[2,300,128]{2,1,0:T(8,128)}, bf16[2,2,2,150,150]{4,3,2,1,0:T(8,128)(2,1)}) custom-call(s32[2]{0:T(128)} %low_ref.1, s32[2]{0:T(128)} %high_ref.1, f32[1024,128]{1,0:T(8,128)} %sum_over_pix.1.packed_ref, f32[300,128]{1,0:T(8,128)} %start_ref.1), custom_call_target="tpu_custom_call" | custom-call | flops 40000000000 | bytes 1000000 | tf_op jit(solution)/shard_map/iterate/pallas_call | solution.py:312
  110.7 1.8 %copy.8 = f32[2,300,128]{2,0,1:T(2,128)} copy(f32[2,300,128]{2,1,0:T(8,128)} %get-tuple-element.13) | data formatting | bytes 614400
  112.6 0.7 collective-permute-done.1.refs_3_
  113.2 0.0 copy-start.2
  113.2 1.1 copy-done.2
  114.4 10.5 %filter.1 = f32[2,4096]{1,0:T(2,128)} custom-call(s32[1]{0:T(128)} %bitcast.place_ref, bf16[2,2,2,150,150]{4,3,2,1,0:T(8,128)(2,1)} %get-tuple-element.7.proj_ref, bf16[2,150,8192]{2,1,0:T(8,128)(2,1)} %reshape.16.own_ref.refs_0_.refs_1_, bf16[2,150,8192]{2,1,0:T(8,128)(2,1)} %reshape.16.own_ref.refs_0_.refs_1_, bf16[150,4096]{1,0:T(8,128)(2,1)} %copy-done, ...), custom_call_target="tpu_custom_call" | custom-call | tf_op jit(solution)/shard_map/filter/pallas_call | solution.py:352
Async XLA Ops:
  6.8 6.5 %copy-start.1 = (bf16[150,2,4096]{2,1,0:T(2,128)(2,1)S(1)}, bf16[150,2,4096]{2,1,0:T(2,128)(2,1)}, u32[]{:S(2)}) copy-start(bf16[150,2,4096]{2,1,0:T(2,128)(2,1)} %param.6) | copy-start | bytes 7372804
  10.4 30.5 %collective-permute-start = (bf16[150,4096]{1,0:T(8,128)(2,1)}, bf16[150,4096]{1,0:T(8,128)(2,1)S(1)}, u32[]{:S(2)}, u32[]{:S(2)}) collective-permute-start(bf16[150,4096]{1,0:T(8,128)(2,1)} %get-tuple-element.14), channel_id=1, source_target_pairs={{0,1},{1,0},{2,3},{3,2},{4,5},{5,4},{6,7},{7,6},{8,9},{9,8},{10,11... | collective-permute-start | bytes 3686408 | tf_op jit(solution)/shard_map/ppermute | solution.py:379
  40.9 1.1 copy-start
  81.7 31.5 %collective-permute-start.1 = (bf16[150,4096]{1,0:T(8,128)(2,1)S(1)}, bf16[150,4096]{1,0:T(8,128)(2,1)S(1)}, u32[]{:S(2)}, u32[]{:S(2)}) collective-permute-start(bf16[150,4096]{1,0:T(8,128)(2,1)S(1)} %get-tuple-element.8), channel_id=1, source_target_pairs={{1,0},{3,2},{5,4},{7,6},{9,8},{11,10},{13,12},{15,14},{17,16},{19,... | collective-permute-start | bytes 3686408 | tf_op jit(solution)/shard_map/ppermute | solution.py:388
  113.2 1.1 copy-start.2

commit v5 on v4

--- a/solution.py
+++ b/solution.py
@@ -11,7 +11,7 @@
 ITERS = 3
 WIN_DEV = 2
 SUB = 8
-PANEL = 4
+PANEL = 8
 LANES = 128
 BLOCKS = 5
 HI = lax.Precision.HIGHEST

time: 126 us -> 126 us (level)
  Pallas kernels: 86.7 us -> 82 us
  waiting for transfers between devices: 13.6 us -> 18.2 us
    pallas_call x1, Pallas kernels: 27.5 us -> 22.9 us  [iterate(): pl.pallas_call(functools.partial(iterate_kernel, half), out_shape=(jax.Sh...]
    ppermute x1, waiting for transfers between devices: 0.69 us -> 5.33 us  [body(): late = lax.ppermute(late, 'tm', [(1, 0)])]
  transfers between devices with their start and end apart: 2 -> 2, of which waited for: 2 -> 2; matrix products, arithmetic and copies ran while one was open for 6% -> 6% of each run, Pallas kernels for 29% -> 25%
where the time goes in v5:
time: 126 us; the launch traced here: 125 us
  Pallas kernels  82 us (65%)
  waiting for transfers between devices  18.2 us (14%)
  local copies, waits for them, and re-layouts  16 us (13%)
  starting transfers between devices  4.44 us (4%)
  other arithmetic  3.55 us (3%)
    pallas_call x1, Pallas kernels, sum_over_pix(): pl.pallas_call(functools.partial(sum_kernel, n, half - LANES), out_shape=...  35.6 us
    pallas_call x1, Pallas kernels, iterate(): pl.pallas_call(functools.partial(iterate_kernel, half), out_shape=(jax.Sh...  22.9 us
    ppermute x1, waiting for transfers between devices, body(): lax.ppermute(jnp.where(front, own[1, :, middle:], own[0, :, :middle]), 't...  12.9 us
    pallas_call x1, Pallas kernels, filtered_power(): pl.pallas_call(functools.partial(filter_kernel, half), out_shape=jax.Shap...  10.5 us
    unnamed x9, local copies, waits for them, and re-layouts  9.82 us
    pallas_call x1, Pallas kernels, gram_blocks(): pl.pallas_call(functools.partial(gram_kernel, half), out_shape=jax.ShapeD...  8.95 us
    reshape x1, local copies, waits for them, and re-layouts, body(): own = iq.reshape(WIN_DEV, half, -1)  6.19 us
    ppermute x1, waiting for transfers between devices, body(): late = lax.ppermute(late, 'tm', [(1, 0)])  5.33 us
  transfers between devices with their start and end apart: 2, of which 2 were waited for; matrix products, arithmetic and copies ran while one was open for 6% of the time, Pallas kernels for 25%

profile of v5, /device:TPU:0, one launch (start us, length us, event | category | flops | bytes accessed | tf_op | source)
XLA Modules:
  0.0 124.9 jit_solution(16400675368678721232)
XLA Ops:
  0.6 6.2 %reshape.16.own_ref.refs_0_.refs_1_ = bf16[2,150,8192]{2,1,0:T(8,128)(2,1)} reshape(bf16[300,2,4096]{2,1,0:T(2,128)(2,1)} %param.5) | data formatting | bytes 9830400 | tf_op jit(solution)/shard_map/reshape | solution.py:377
  6.8 0.0 copy-start.1
  6.8 3.5 %fusion = (bf16[150,4096]{1,0:T(8,128)(2,1)}, bf16[150,4096]{1,0:T(8,128)(2,1)S(1)}) fusion(bf16[2,150,8192]{2,1,0:T(8,128)(2,1)} %reshape.16.own_ref.refs_0_.refs_1_, pred[]{:T(512)S(6)} %eq.3), kind=kLoop, calls=%fused_computation.1 | loop fusion | flops 614400 | bytes 6144001 | tf_op jit(solution)/shard_map/jit(_where)/select_n | solution.py:380
  10.4 3.0 %collective-permute-start = (bf16[150,4096]{1,0:T(8,128)(2,1)}, bf16[150,4096]{1,0:T(8,128)(2,1)S(1)}, u32[]{:S(2)}, u32[]{:S(2)}) collective-permute-start(bf16[150,4096]{1,0:T(8,128)(2,1)} %get-tuple-element.14), channel_id=1, source_target_pairs={{0,1},{1,0},{2,3},{3,2},{4,5},{5,4},{6,7},{7,6},{8,9},{9,8},{10,11... | collective-permute-start | bytes 3686408 | tf_op jit(solution)/shard_map/ppermute | solution.py:379
  13.3 0.0 copy-done.1
  13.3 2.6 %pad = bf16[152,2,4096]{2,1,0:T(2,128)(2,1)S(1)} pad(bf16[150,2,4096]{2,1,0:T(2,128)(2,1)S(1)} %copy-done.1, bf16[]{:T(256)} %constant.6), padding=0_2x0_0x0_0 | pad | bytes 4947970
  16.0 3.1 %copy.9 = bf16[19,8,2,4096]{3,1,2,0:T(8,128)(2,1)} copy(bf16[19,8,2,4096]{3,2,1,0:T(2,128)(2,1)S(1)} %bitcast.11) | data formatting | bytes 4980736
  19.1 9.0 %gram.1.packed_ref.x_ref = f32[1024,128]{1,0:T(8,128)} custom-call(bf16[2,150,8192]{2,1,0:T(8,128)(2,1)} %reshape.16.own_ref.refs_0_.refs_1_, bf16[150,8192]{1,0:T(8,128)(2,1)} %bitcast.8), custom_call_target="tpu_custom_call" | custom-call | tf_op jit(solution)/shard_map/gram/pallas_call | solution.py:59
  28.0 12.9 %collective-permute-done.swapped_ref.refs_2_ = bf16[150,4096]{1,0:T(8,128)(2,1)S(1)} collective-permute-done((bf16[150,4096]{1,0:T(8,128)(2,1)}, bf16[150,4096]{1,0:T(8,128)(2,1)S(1)}, u32[]{:S(2)}, u32[]{:S(2)}) %collective-permute-start) | collective-permute-done | bytes 1228832 | tf_op jit(solution)/shard_map/ppermute | solution.py:379
  40.9 0.0 copy-start
  40.9 1.1 copy-done
  42.1 4.0 %cross.1.extra_ref = f32[456,128]{1,0:T(8,128)} custom-call(s32[1]{0:T(128)} %bitcast.place_ref, bf16[2,150,8192]{2,1,0:T(8,128)(2,1)} %reshape.16.own_ref.refs_0_.refs_1_, bf16[150,4096]{1,0:T(8,128)(2,1)} %copy-done, f32[1024,128]{1,0:T(8,128)} %gram.1.packed_ref.x_ref), custom_call_target="tpu_custom_call" | custom-call | tf_op jit(solution)/shard_map/cross/pallas_call | solution.py:109
  46.1 35.6 %sum_over_pix.1.packed_ref = f32[1024,128]{1,0:T(8,128)} custom-call(f32[1024,128]{1,0:T(8,128)} %gram.1.packed_ref.x_ref, f32[456,128]{1,0:T(8,128)} %cross.1.extra_ref), custom_call_target="tpu_custom_call" | custom-call | tf_op jit(solution)/shard_map/sum_over_pix/pallas_call | solution.py:208
  81.7 1.5 %collective-permute-start.1 = (bf16[150,4096]{1,0:T(8,128)(2,1)S(1)}, bf16[150,4096]{1,0:T(8,128)(2,1)S(1)}, u32[]{:S(2)}, u32[]{:S(2)}) collective-permute-start(bf16[150,4096]{1,0:T(8,128)(2,1)S(1)} %get-tuple-element.8), channel_id=1, source_target_pairs={{1,0},{3,2},{5,4},{7,6},{9,8},{11,10},{13,12},{15,14},{17,16},{19,... | collective-permute-start | bytes 3686408 | tf_op jit(solution)/shard_map/ppermute | solution.py:388
  83.2 22.9 %iterate.1 = (f32[2,300,128]{2,1,0:T(8,128)}, bf16[2,2,2,150,150]{4,3,2,1,0:T(8,128)(2,1)}) custom-call(s32[2]{0:T(128)} %low_ref.1, s32[2]{0:T(128)} %high_ref.1, f32[1024,128]{1,0:T(8,128)} %sum_over_pix.1.packed_ref, f32[300,128]{1,0:T(8,128)} %start_ref.1), custom_call_target="tpu_custom_call" | custom-call | flops 40000000000 | bytes 1000000 | tf_op jit(solution)/shard_map/iterate/pallas_call | solution.py:312
  106.1 1.8 %copy.8 = f32[2,300,128]{2,0,1:T(2,128)} copy(f32[2,300,128]{2,1,0:T(8,128)} %get-tuple-element.13) | data formatting | bytes 614400
  107.9 5.3 %collective-permute-done.1.refs_3_ = bf16[150,4096]{1,0:T(8,128)(2,1)S(1)} collective-permute-done((bf16[150,4096]{1,0:T(8,128)(2,1)S(1)}, bf16[150,4096]{1,0:T(8,128)(2,1)S(1)}, u32[]{:S(2)}, u32[]{:S(2)}) %collective-permute-start.1) | collective-permute-done | bytes 1228832 | tf_op jit(solution)/shard_map/ppermute | solution.py:388
  113.2 0.0 copy-start.2
  113.2 1.1 copy-done.2
  114.4 10.5 %filter.1 = f32[2,4096]{1,0:T(2,128)} custom-call(s32[1]{0:T(128)} %bitcast.place_ref, bf16[2,2,2,150,150]{4,3,2,1,0:T(8,128)(2,1)} %get-tuple-element.7.proj_ref, bf16[2,150,8192]{2,1,0:T(8,128)(2,1)} %reshape.16.own_ref.refs_0_.refs_1_, bf16[2,150,8192]{2,1,0:T(8,128)(2,1)} %reshape.16.own_ref.refs_0_.refs_1_, bf16[150,4096]{1,0:T(8,128)(2,1)} %copy-done, ...), custom_call_target="tpu_custom_call" | custom-call | tf_op jit(solution)/shard_map/filter/pallas_call | solution.py:352
Async XLA Ops:
  6.8 6.5 %copy-start.1 = (bf16[150,2,4096]{2,1,0:T(2,128)(2,1)S(1)}, bf16[150,2,4096]{2,1,0:T(2,128)(2,1)}, u32[]{:S(2)}) copy-start(bf16[150,2,4096]{2,1,0:T(2,128)(2,1)} %param.6) | copy-start | bytes 7372804
  10.4 30.5 %collective-permute-start = (bf16[150,4096]{1,0:T(8,128)(2,1)}, bf16[150,4096]{1,0:T(8,128)(2,1)S(1)}, u32[]{:S(2)}, u32[]{:S(2)}) collective-permute-start(bf16[150,4096]{1,0:T(8,128)(2,1)} %get-tuple-element.14), channel_id=1, source_target_pairs={{0,1},{1,0},{2,3},{3,2},{4,5},{5,4},{6,7},{7,6},{8,9},{9,8},{10,11... | collective-permute-start | bytes 3686408 | tf_op jit(solution)/shard_map/ppermute | solution.py:379
  40.9 1.1 copy-start
  81.7 31.5 %collective-permute-start.1 = (bf16[150,4096]{1,0:T(8,128)(2,1)S(1)}, bf16[150,4096]{1,0:T(8,128)(2,1)S(1)}, u32[]{:S(2)}, u32[]{:S(2)}) collective-permute-start(bf16[150,4096]{1,0:T(8,128)(2,1)S(1)} %get-tuple-element.8), channel_id=1, source_target_pairs={{1,0},{3,2},{5,4},{7,6},{9,8},{11,10},{13,12},{15,14},{17,16},{19,... | collective-permute-start | bytes 3686408 | tf_op jit(solution)/shard_map/ppermute | solution.py:388
  113.2 1.1 copy-start.2
